TPU v7x, 1024 devices: a whole 4x4x32 slice. The times are simulated.
1024 devices in a mesh: gx: 32 (over z), gy: 8 (over x, core), gz: 4 (over y).
Axes of the slice: x: 4, y: 4, z: 32, core: 2. Of those that a mesh axis runs over, the one named last changes fastest.
Arguments:
- pops: float32 [19, 32, 64, 4096], P(None, 'gz', 'gy', 'gx'), may hold values from 0.4 to 1.6
- coarse_pops: bfloat16 [19, 32, 64, 4096], P(None, 'gz', 'gy', 'gx'), may hold values from 0.3984375 to 1.59375
- interface: int32 [32, 64, 4096], P('gz', 'gy', 'gx'), may hold values 0 or 1
- drop_vel: float32 [3, 16384, 128], P(None, ('gx', 'gy', 'gz')), may hold values from -1 to 1
- drop_frac: float32 [3, 16384, 128], P(None, ('gx', 'gy', 'gz')), may hold values from 0 to 1
- home: int32 [16384, 128], P(('gx', 'gy', 'gz')), may hold values from 0 to 8191, as said below
- counts: int32 [16384], P(('gx', 'gy', 'gz')), may hold values from 1 to 128, 1572864 in all
- dest: int32 [16384], P(('gx', 'gy', 'gz')), may hold values from 0 to 26, as said below
Outputs:
- pops_out: float32 [19, 32, 64, 4096], P(None, 'gz', 'gy', 'gx')
- force: float32 [3, 32, 64, 4096], P(None, 'gz', 'gy', 'gx')
- arrived: float32 [6, 69632, 128], P(None, ('gx', 'gy', 'gz'))
Inputs may be any that keep to these rules, and one draw needn't show every extreme that they name: All droplets of a block lie in one tile of 8 x 8 x 8 cells at tile-aligned offsets; home = (8 * z + y) * 128 + x in the device's brick. `counts`: live droplets fill the first slots of their block. `dest`: no block crosses a wall along z; apart from code 13, at most 2 blocks of one device share a code, and every device has exactly 2 blocks of some code other than 13.
All inputs are finite; a program needn't handle non-finite values. No bound on the sum of `interface` on one device may be relied on, other than what follows from the above.
Results may differ from a plain program's by a relative error of at most 0.0003.
Values sent between devices are 32-bit elements; how exact they have to be, the bound alone decides.
A program may use at most 32 MiB of HBM per device.

v0:
```python
import math

import jax
import jax.numpy as jnp
import numpy as np
from jax import lax
from jax.sharding import PartitionSpec as P

TILE = 8
CAP = 2


lattice = np.array(
    [
        [0, 0, 0],
        [1, 0, 0],
        [-1, 0, 0],
        [0, 1, 0],
        [0, -1, 0],
        [0, 0, 1],
        [0, 0, -1],
        [1, 1, 0],
        [-1, -1, 0],
        [1, -1, 0],
        [-1, 1, 0],
        [1, 0, 1],
        [-1, 0, -1],
        [1, 0, -1],
        [-1, 0, 1],
        [0, 1, 1],
        [0, -1, -1],
        [0, 1, -1],
        [0, -1, 1],
    ]
)
weights_table = np.array([1.0 / 3.0] + [1.0 / 18.0] * 6 + [1.0 / 36.0] * 12)
opposite = [0, 2, 1, 4, 3, 6, 5, 8, 7, 10, 9, 12, 11, 14, 13, 16, 15, 18, 17]
inverse_tau = 0.8
relax = 0.5
couple = 8.0
highest = lax.Precision.HIGHEST


def with_halo(cells, sides, width):
    for axis, dim in sides:
        count = lax.axis_size(axis)
        head = lax.slice_in_dim(cells, 0, width, axis=dim)
        tail = lax.slice_in_dim(cells, cells.shape[dim] - width, cells.shape[dim], axis=dim)
        cells = jnp.concatenate(
            [
                lax.ppermute(tail, axis, [(i, (i + 1) % count) for i in range(count)]),
                cells,
                lax.ppermute(head, axis, [((i + 1) % count, i) for i in range(count)]),
            ],
            axis=dim,
        )
    return cells


def kernel(distance):
    return 0.25 * (1.0 + jnp.cos(math.pi * 0.5 * distance))


def macroscopic(pops):
    density = pops[0] * float(weights_table[0])
    moment = [jnp.zeros_like(density), jnp.zeros_like(density), jnp.zeros_like(density)]
    for index in range(1, 19):
        term = pops[index] * float(weights_table[index])
        density = density + term
        for axis in range(3):
            if int(lattice[index][axis]) != 0:
                moment[axis] = moment[axis] + float(lattice[index][axis]) * term
    return (density, [moment[axis] / density for axis in range(3)])


def collide(pops, coarse, interface):
    density, flow = macroscopic(pops)
    square = flow[0] * flow[0] + flow[1] * flow[1] + flow[2] * flow[2]
    inside = interface == 1
    posts = []
    for index in range(19):
        along = jnp.zeros_like(density)
        for axis in range(3):
            if int(lattice[index][axis]) != 0:
                along = along + float(lattice[index][axis]) * flow[axis]
        balance = density * (1.0 + 3.0 * along + 4.5 * along * along - 1.5 * square)
        relaxed = pops[index] - (pops[index] - balance) * inverse_tau
        posts.append(jnp.where(inside, coarse[index].astype(jnp.float32), relaxed))
    return jnp.stack(posts)


def window(source, index, grown, shape):
    starts = [
        grown[0] * (1 - int(lattice[index][2])),
        grown[1] * (1 - int(lattice[index][1])),
        grown[2] * (1 - int(lattice[index][0])),
    ]
    return source[
        starts[0] : starts[0] + shape[0],
        starts[1] : starts[1] + shape[1],
        starts[2] : starts[2] + shape[2],
    ]


def joint_pull(posts):
    shape = posts.shape[1:]
    extended = with_halo(posts, (("gx", 3), ("gy", 2), ("gz", 1)), 1)
    return [window(extended[index], index, (1, 1, 1), shape) for index in range(19)]


def wall_fix(pulled, posts, bottom, top):
    fixed = []
    for index in range(19):
        value = pulled[index]
        if int(lattice[index][2]) == 1:
            value = jnp.where(bottom, posts[opposite[index]], value)
        if int(lattice[index][2]) == -1:
            value = jnp.where(top, posts[opposite[index]], value)
        fixed.append(value)
    return jnp.stack(fixed)


def row_weights(offset, frac):
    span = lax.broadcasted_iota(jnp.int32, (1, TILE + 4), 1)
    distance = span - 2 - offset[:, None] - frac[:, None]
    return jnp.where(jnp.abs(distance) < 2.0, kernel(distance), 0.0)


def fold(array, dim, inner):
    core = lax.slice_in_dim(array, 4, inner + 4, axis=dim)
    lower = lax.slice_in_dim(array, 0, 2, axis=dim)
    upper = lax.slice_in_dim(array, inner + 6, inner + 8, axis=dim)
    low_pad = [(0, 0)] * array.ndim
    high_pad = [(0, 0)] * array.ndim
    low_pad[dim] = (0, inner - 2)
    high_pad[dim] = (inner - 2, 0)
    return core + jnp.pad(lower, low_pad) + jnp.pad(upper, high_pad)


def local(pops, coarse_pops, interface, drop_vel, drop_frac, home, counts, dest):
    level = lax.axis_index("gz")
    levels = lax.axis_size("gz")
    depth, height, width = interface.shape
    rows = lax.broadcasted_iota(jnp.int32, (depth, 1, 1), 0)
    bottom = (level == 0) & (rows == 0)
    top = (level == levels - 1) & (rows == depth - 1)
    state = pops
    for substep in range(2):
        posts = collide(state, coarse_pops, interface)
        pulled = joint_pull(posts)
        state = wall_fix(pulled, posts, bottom, top)
    density, flow = macroscopic(state)
    velocity = jnp.stack(flow)
    velocity_ext = with_halo(velocity, (("gx", 3), ("gy", 2), ("gz", 1)), 2)
    rim_rows = lax.broadcasted_iota(jnp.int32, (1, depth + 4, 1, 1), 1)
    keep = jnp.logical_not(
        (level == 0) & (rim_rows < 2) | (level == levels - 1) & (rim_rows >= depth + 2)
    )
    velocity_ext = jnp.where(keep, velocity_ext, 0.0)
    blocks = home.shape[0]
    groups = blocks // 4
    edge = TILE + 4
    homes = home.reshape(groups, 4, 128)
    speeds = jnp.moveaxis(drop_vel, 1, 0).reshape(groups, 4, 3, 128)
    fracs = jnp.moveaxis(drop_frac, 1, 0).reshape(groups, 4, 3, 128)
    slots = lax.broadcasted_iota(jnp.int32, (blocks, 128), 1)
    lives = (slots < counts[:, None]).reshape(groups, 4, 128)

    def droplet_group(spread, group):
        group_homes, group_speeds, group_fracs, group_lives = group
        results = []
        for member in range(4):
            cells = group_homes[member]
            speed = group_speeds[member]
            frac = group_fracs[member]
            alive = group_lives[member][None, :]
            first = cells[0]
            start_x = first % width // TILE * TILE
            start_y = first // width % height // TILE * TILE
            start_z = first // (width * height) // TILE * TILE
            weight_x = row_weights(cells % width - start_x, frac[0])
            weight_y = row_weights(cells // width % height - start_y, frac[1])
            weight_z = row_weights(cells // (width * height) - start_z, frac[2])
            corner = (jnp.zeros((), jnp.int32), start_z, start_y, start_x)
            tile = lax.dynamic_slice(velocity_ext, corner, (3, edge, edge, edge))
            partial_value = jnp.dot(
                tile.reshape(3 * edge * edge, edge), weight_x.T, precision=highest
            )
            partial_value = jnp.sum(
                partial_value.reshape(3, edge, edge, 128) * weight_y.T[None, None, :, :], axis=2
            )
            sampled = jnp.sum(partial_value * weight_z.T[None, :, :], axis=1)
            moved = speed + relax * (sampled - speed)
            push = jnp.where(alive, couple * (moved - sampled), 0.0)
            source = (
                push[:, None, None, :] * weight_z.T[None, :, None, :] * weight_y.T[None, None, :, :]
            )
            patch = jnp.dot(source.reshape(3 * edge * edge, 128), weight_x, precision=highest)
            patch = patch.reshape(3, edge, edge, edge)
            spread = lax.dynamic_update_slice(
                spread, lax.dynamic_slice(spread, corner, (3, edge, edge, edge)) + patch, corner
            )
            results.append(jnp.where(alive, jnp.concatenate([moved, frac + moved], axis=0), 0.0))
        return (spread, jnp.stack(results))

    spread, states = lax.scan(
        droplet_group, jnp.zeros_like(velocity_ext), (homes, speeds, fracs, lives)
    )
    states = jnp.moveaxis(states.reshape(blocks, 6, 128), 0, 1)
    spread = jnp.where(keep, spread, 0.0)
    force_ext = with_halo(spread, (("gx", 3), ("gy", 2), ("gz", 1)), 2)
    force = fold(fold(fold(force_ext, 1, depth), 2, height), 3, width)
    order = lax.broadcasted_iota(jnp.int32, (blocks,), 0)
    earlier = (dest[:, None] == dest[None, :]) & (order[None, :] < order[:, None])
    rank = jnp.sum(earlier.astype(jnp.int32), axis=1)
    moving = dest != 13
    slot = jnp.where(moving, dest * CAP + rank, 27 * CAP)
    outbox = jnp.zeros((6, 27 * CAP, 128), jnp.float32).at[:, slot].set(states, mode="drop")
    outbox = outbox.reshape(6, 3, 3, 3, CAP, 128)
    arrived_box = with_halo(outbox, (("gx", 3), ("gy", 2), ("gz", 1)), 1)
    inbox = arrived_box[:, 4::-2, 4::-2, 4::-2].reshape(6, 27 * CAP, 128)
    incoming = jnp.concatenate([inbox[:, : 13 * CAP], inbox[:, 14 * CAP :]], axis=1)
    staying = jnp.where(moving[None, :, None], 0.0, states)
    arrived = jnp.concatenate([staying, incoming], axis=1)
    return (state, force, arrived)


def solution(mesh):
    return jax.shard_map(
        local,
        mesh=mesh,
        in_specs=(
            P(None, "gz", "gy", "gx"),
            P(None, "gz", "gy", "gx"),
            P("gz", "gy", "gx"),
            P(None, ("gx", "gy", "gz"), None),
            P(None, ("gx", "gy", "gz"), None),
            P(("gx", "gy", "gz"), None),
            P(("gx", "gy", "gz")),
            P(("gx", "gy", "gz")),
        ),
        out_specs=(
            P(None, "gz", "gy", "gx"),
            P(None, "gz", "gy", "gx"),
            P(None, ("gx", "gy", "gz"), None),
        ),
        check_vma=False,
    )
```

profile of v0, /device:TPU:1, one launch (start us, length us, event | category | flops | bytes accessed | tf_op | source)
XLA Modules:
  0.0 325.1 jit_solution(3719359287927214399)
XLA Ops:
  0.6 1.2 constant_dynamic-update-slice_fusion.18
  16.9 4.4 %collective-permute-start = (f32[19,8,8,1]{0,2,3,1:T(8,128)S(1)}, f32[19,8,8,1]{0,2,3,1:T(8,128)S(1)}, u32[]{:S(2)}, u32[]{:S(2)}) collective-permute-start(f32[19,8,8,1]{0,2,3,1:T(8,128)S(1)} %copy.119), channel_id=1, source_target_pairs={{0,32},{32,64},{64,96},{96,128},{128,160},{160,192},{192,224},{224... | collective-permute-start | bytes 14600 | tf_op jit(solution)/shard_map/ppermute | solution.py:51
  21.8 16.8 %collective-permute-start.1 = (f32[19,8,8,1]{0,2,3,1:T(8,128)S(1)}, f32[19,8,8,1]{0,2,3,1:T(8,128)S(1)}, u32[]{:S(2)}, u32[]{:S(2)}) collective-permute-start(f32[19,8,8,1]{0,2,3,1:T(8,128)S(1)} %copy.120), channel_id=1, source_target_pairs={{32,0},{64,32},{96,64},{128,96},{160,128},{192,160},{224,192},{256... | collective-permute-start | bytes 14600 | tf_op jit(solution)/shard_map/ppermute | solution.py:53
  40.3 1.1 pad_maximum_fusion.25
  41.4 2.6 collective-permute-start.2
  44.2 2.0 collective-permute-done.2
  46.2 2.5 collective-permute-done.3
  49.0 3.2 collective-permute-start.4
  52.2 3.4 %collective-permute-start.5 = (f32[19,1,10,130]{3,2,1,0:T(8,128)S(1)}, f32[19,1,10,130]{3,2,1,0:T(8,128)S(1)}, u32[]{:S(2)}, u32[]{:S(2)}) collective-permute-start(f32[19,1,10,130]{3,2,1,0:T(8,128)S(1)} %get-tuple-element.376), channel_id=1, source_target_pairs={{1,0},{2,1},{3,2},{0,3},{5,4},{6,5},{7,6},{4,7},{9,8},{10,9},{11,1... | collective-permute-start | bytes 296408 | tf_op jit(solution)/shard_map/ppermute | solution.py:53
  55.6 5.5 %collective-permute-done.4 = f32[19,1,10,130]{3,2,1,0:T(8,128)S(1)} collective-permute-done((f32[19,1,10,130]{3,2,1,0:T(8,128)S(1)}, f32[19,1,10,130]{3,2,1,0:T(8,128)S(1)}, u32[]{:S(2)}, u32[]{:S(2)}) %collective-permute-start.4) | collective-permute-done | bytes 98832 | tf_op jit(solution)/shard_map/ppermute | solution.py:51
  61.0 1.6 collective-permute-done.5
  62.6 1.2 pad_maximum_fusion
  66.3 1.9 collective-permute-start.6
  68.8 5.2 %collective-permute-start.7 = (f32[19,8,8,1]{0,2,3,1:T(8,128)S(1)}, f32[19,8,8,1]{0,2,3,1:T(8,128)S(1)}, u32[]{:S(2)}, u32[]{:S(2)}) collective-permute-start(f32[19,8,8,1]{0,2,3,1:T(8,128)S(1)} %copy.124), channel_id=1, source_target_pairs={{32,0},{64,32},{96,64},{128,96},{160,128},{192,160},{224,192},{256... | collective-permute-start | bytes 14600 | tf_op jit(solution)/shard_map/ppermute | solution.py:53
  75.6 1.0 pad_maximum_fusion.22
  76.7 2.5 collective-permute-start.8
  79.3 2.1 collective-permute-done.8
  81.4 2.8 collective-permute-done.9
  84.5 3.2 collective-permute-start.10
  87.7 3.5 %collective-permute-start.11 = (f32[19,1,10,130]{3,2,1,0:T(8,128)S(1)}, f32[19,1,10,130]{3,2,1,0:T(8,128)S(1)}, u32[]{:S(2)}, u32[]{:S(2)}) collective-permute-start(f32[19,1,10,130]{3,2,1,0:T(8,128)S(1)} %get-tuple-element.374), channel_id=1, source_target_pairs={{1,0},{2,1},{3,2},{0,3},{5,4},{6,5},{7,6},{4,7},{9,8},{10,9},{11,1... | collective-permute-start | bytes 296408 | tf_op jit(solution)/shard_map/ppermute | solution.py:53
  91.2 4.8 %collective-permute-done.10 = f32[19,1,10,130]{3,2,1,0:T(8,128)S(1)} collective-permute-done((f32[19,1,10,130]{3,2,1,0:T(8,128)S(1)}, f32[19,1,10,130]{3,2,1,0:T(8,128)S(1)}, u32[]{:S(2)}, u32[]{:S(2)}) %collective-permute-start.10) | collective-permute-done | bytes 98832 | tf_op jit(solution)/shard_map/ppermute | solution.py:51
  95.9 1.7 collective-permute-done.11
  97.7 1.2 pad_maximum_fusion.1
  99.9 1.9 collective-permute-start.12
  101.8 5.2 %collective-permute-start.13 = (f32[3,8,8,2]{3,2,1,0:T(8,128)S(1)}, f32[3,8,8,2]{3,2,1,0:T(8,128)S(1)}, u32[]{:S(2)}, u32[]{:S(2)}) collective-permute-start(f32[3,8,8,2]{3,2,1,0:T(8,128)S(1)} %get-tuple-element.406), channel_id=1, source_target_pairs={{32,0},{64,32},{96,64},{128,96},{160,128},{192,160},{224,192},{256... | collective-permute-start | bytes 4616 | tf_op jit(solution)/shard_map/ppermute | solution.py:53
  107.5 1.1 collective-permute-done.13
  108.8 2.8 collective-permute-start.14
  111.6 1.2 collective-permute-done.14
  112.8 2.6 collective-permute-done.15
  115.6 2.9 collective-permute-start.16
  118.5 3.6 %collective-permute-start.17 = (f32[3,2,12,132]{3,2,1,0:T(8,128)S(1)}, f32[3,2,12,132]{3,2,1,0:T(8,128)S(1)}, u32[]{:S(2)}, u32[]{:S(2)}) collective-permute-start(f32[3,2,12,132]{3,2,1,0:T(8,128)S(1)} %get-tuple-element.394), channel_id=1, source_target_pairs={{1,0},{2,1},{3,2},{0,3},{5,4},{6,5},{7,6},{4,7},{9,8},{10,9},{11,1... | collective-permute-start | bytes 114056 | tf_op jit(solution)/shard_map/ppermute | solution.py:53
  122.2 1.7 collective-permute-done.17
  124.2 156.9 %while.15 = (s32[]{:T(128)}, f32[3,12,12,132]{3,2,1,0:T(8,128)S(1)}, f32[4,4,6,128]{3,1,0,2:T(4,128)S(1)}, s32[4,4,128]{2,1,0:T(4,128)}, pred[4,4,128]{2,1,0:T(4...) while((s32[]{:T(128)}, ...), condition=%wide.region_9.10_spmd, body=%wide.region_0.9_spmd.sunk | while | flops 64692984 | bytes 2140945 | solution.py:206
  139.5 5.5 %dynamic_update_slice.47 = f32[3,12,12,132]{3,2,1,0:T(8,128)S(1)} dynamic-update-slice(f32[3,12,12,132]{3,2,1,0:T(8,128)S(1)} %get-tuple-element.593, f32[3,12,12,12]{3,2,1,0:T(8,128)S(1)} %convolution_add_fusion.8, s32[]{:T(128)} %constant.666.clone.1..sunk, s32[]{:T(128)} %constant.666.clone.1..sunk, s32[]{:T(128)} %constant.666.clone.1..sunk, s32[]{:T(128)S(6)} %select_n.1304) | dynamic-update-slice | bytes 41476 | tf_op jit(solution)/shard_map/while/body/eval_jaxpr/dynamic_update_slice | solution.py:200
  145.6 5.5 %dynamic_update_slice.48 = f32[3,12,12,132]{3,2,1,0:T(8,128)S(1)} dynamic-update-slice(f32[3,12,12,132]{3,2,1,0:T(8,128)S(1)} %dynamic_update_slice.47, f32[3,12,12,12]{3,2,1,0:T(8,128)S(1)} %convolution_add_fusion.9, s32[]{:T(128)} %constant.666.clone.1..sunk, s32[]{:T(128)} %constant.666.clone.1..sunk, s32[]{:T(128)} %constant.666.clone.1..sunk, s32[]{:T(128)S(6)} %select_n.1307) | dynamic-update-slice | bytes 41476 | tf_op jit(solution)/shard_map/while/body/eval_jaxpr/dynamic_update_slice | solution.py:200
  151.7 5.5 %dynamic_update_slice.49 = f32[3,12,12,132]{3,2,1,0:T(8,128)S(1)} dynamic-update-slice(f32[3,12,12,132]{3,2,1,0:T(8,128)S(1)} %dynamic_update_slice.48, f32[3,12,12,12]{3,2,1,0:T(8,128)S(1)} %convolution_add_fusion.10, s32[]{:T(128)} %constant.666.clone.1..sunk, s32[]{:T(128)} %constant.666.clone.1..sunk, s32[]{:T(128)} %constant.666.clone.1..sunk, s32[]{:T(128)S(6)} %select_n.1333) | dynamic-update-slice | bytes 41476 | tf_op jit(solution)/shard_map/while/body/eval_jaxpr/dynamic_update_slice | solution.py:200
  157.8 5.5 %dynamic_update_slice.50 = f32[3,12,12,132]{3,2,1,0:T(8,128)S(1)} dynamic-update-slice(f32[3,12,12,132]{3,2,1,0:T(8,128)S(1)} %dynamic_update_slice.49, f32[3,12,12,12]{3,2,1,0:T(8,128)S(1)} %convolution_add_fusion.11, s32[]{:T(128)} %constant.666.clone.1..sunk, s32[]{:T(128)} %constant.666.clone.1..sunk, s32[]{:T(128)} %constant.666.clone.1..sunk, s32[]{:T(128)S(6)} %select_n.1332) | dynamic-update-slice | bytes 41476 | tf_op jit(solution)/shard_map/while/body/eval_jaxpr/dynamic_update_slice | solution.py:200
  178.8 5.5 %dynamic_update_slice.47 = f32[3,12,12,132]{3,2,1,0:T(8,128)S(1)} dynamic-update-slice(f32[3,12,12,132]{3,2,1,0:T(8,128)S(1)} %get-tuple-element.593, f32[3,12,12,12]{3,2,1,0:T(8,128)S(1)} %convolution_add_fusion.8, s32[]{:T(128)} %constant.666.clone.1..sunk, s32[]{:T(128)} %constant.666.clone.1..sunk, s32[]{:T(128)} %constant.666.clone.1..sunk, s32[]{:T(128)S(6)} %select_n.1304) | dynamic-update-slice | bytes 41476 | tf_op jit(solution)/shard_map/while/body/eval_jaxpr/dynamic_update_slice | solution.py:200
  184.8 5.5 %dynamic_update_slice.48 = f32[3,12,12,132]{3,2,1,0:T(8,128)S(1)} dynamic-update-slice(f32[3,12,12,132]{3,2,1,0:T(8,128)S(1)} %dynamic_update_slice.47, f32[3,12,12,12]{3,2,1,0:T(8,128)S(1)} %convolution_add_fusion.9, s32[]{:T(128)} %constant.666.clone.1..sunk, s32[]{:T(128)} %constant.666.clone.1..sunk, s32[]{:T(128)} %constant.666.clone.1..sunk, s32[]{:T(128)S(6)} %select_n.1307) | dynamic-update-slice | bytes 41476 | tf_op jit(solution)/shard_map/while/body/eval_jaxpr/dynamic_update_slice | solution.py:200
  190.9 5.5 %dynamic_update_slice.49 = f32[3,12,12,132]{3,2,1,0:T(8,128)S(1)} dynamic-update-slice(f32[3,12,12,132]{3,2,1,0:T(8,128)S(1)} %dynamic_update_slice.48, f32[3,12,12,12]{3,2,1,0:T(8,128)S(1)} %convolution_add_fusion.10, s32[]{:T(128)} %constant.666.clone.1..sunk, s32[]{:T(128)} %constant.666.clone.1..sunk, s32[]{:T(128)} %constant.666.clone.1..sunk, s32[]{:T(128)S(6)} %select_n.1333) | dynamic-update-slice | bytes 41476 | tf_op jit(solution)/shard_map/while/body/eval_jaxpr/dynamic_update_slice | solution.py:200
  197.0 5.5 %dynamic_update_slice.50 = f32[3,12,12,132]{3,2,1,0:T(8,128)S(1)} dynamic-update-slice(f32[3,12,12,132]{3,2,1,0:T(8,128)S(1)} %dynamic_update_slice.49, f32[3,12,12,12]{3,2,1,0:T(8,128)S(1)} %convolution_add_fusion.11, s32[]{:T(128)} %constant.666.clone.1..sunk, s32[]{:T(128)} %constant.666.clone.1..sunk, s32[]{:T(128)} %constant.666.clone.1..sunk, s32[]{:T(128)S(6)} %select_n.1332) | dynamic-update-slice | bytes 41476 | tf_op jit(solution)/shard_map/while/body/eval_jaxpr/dynamic_update_slice | solution.py:200
  218.0 5.5 %dynamic_update_slice.47 = f32[3,12,12,132]{3,2,1,0:T(8,128)S(1)} dynamic-update-slice(f32[3,12,12,132]{3,2,1,0:T(8,128)S(1)} %get-tuple-element.593, f32[3,12,12,12]{3,2,1,0:T(8,128)S(1)} %convolution_add_fusion.8, s32[]{:T(128)} %constant.666.clone.1..sunk, s32[]{:T(128)} %constant.666.clone.1..sunk, s32[]{:T(128)} %constant.666.clone.1..sunk, s32[]{:T(128)S(6)} %select_n.1304) | dynamic-update-slice | bytes 41476 | tf_op jit(solution)/shard_map/while/body/eval_jaxpr/dynamic_update_slice | solution.py:200
  224.0 5.5 %dynamic_update_slice.48 = f32[3,12,12,132]{3,2,1,0:T(8,128)S(1)} dynamic-update-slice(f32[3,12,12,132]{3,2,1,0:T(8,128)S(1)} %dynamic_update_slice.47, f32[3,12,12,12]{3,2,1,0:T(8,128)S(1)} %convolution_add_fusion.9, s32[]{:T(128)} %constant.666.clone.1..sunk, s32[]{:T(128)} %constant.666.clone.1..sunk, s32[]{:T(128)} %constant.666.clone.1..sunk, s32[]{:T(128)S(6)} %select_n.1307) | dynamic-update-slice | bytes 41476 | tf_op jit(solution)/shard_map/while/body/eval_jaxpr/dynamic_update_slice | solution.py:200
  230.1 5.5 %dynamic_update_slice.49 = f32[3,12,12,132]{3,2,1,0:T(8,128)S(1)} dynamic-update-slice(f32[3,12,12,132]{3,2,1,0:T(8,128)S(1)} %dynamic_update_slice.48, f32[3,12,12,12]{3,2,1,0:T(8,128)S(1)} %convolution_add_fusion.10, s32[]{:T(128)} %constant.666.clone.1..sunk, s32[]{:T(128)} %constant.666.clone.1..sunk, s32[]{:T(128)} %constant.666.clone.1..sunk, s32[]{:T(128)S(6)} %select_n.1333) | dynamic-update-slice | bytes 41476 | tf_op jit(solution)/shard_map/while/body/eval_jaxpr/dynamic_update_slice | solution.py:200
  236.2 5.5 %dynamic_update_slice.50 = f32[3,12,12,132]{3,2,1,0:T(8,128)S(1)} dynamic-update-slice(f32[3,12,12,132]{3,2,1,0:T(8,128)S(1)} %dynamic_update_slice.49, f32[3,12,12,12]{3,2,1,0:T(8,128)S(1)} %convolution_add_fusion.11, s32[]{:T(128)} %constant.666.clone.1..sunk, s32[]{:T(128)} %constant.666.clone.1..sunk, s32[]{:T(128)} %constant.666.clone.1..sunk, s32[]{:T(128)S(6)} %select_n.1332) | dynamic-update-slice | bytes 41476 | tf_op jit(solution)/shard_map/while/body/eval_jaxpr/dynamic_update_slice | solution.py:200
  257.2 5.5 %dynamic_update_slice.47 = f32[3,12,12,132]{3,2,1,0:T(8,128)S(1)} dynamic-update-slice(f32[3,12,12,132]{3,2,1,0:T(8,128)S(1)} %get-tuple-element.593, f32[3,12,12,12]{3,2,1,0:T(8,128)S(1)} %convolution_add_fusion.8, s32[]{:T(128)} %constant.666.clone.1..sunk, s32[]{:T(128)} %constant.666.clone.1..sunk, s32[]{:T(128)} %constant.666.clone.1..sunk, s32[]{:T(128)S(6)} %select_n.1304) | dynamic-update-slice | bytes 41476 | tf_op jit(solution)/shard_map/while/body/eval_jaxpr/dynamic_update_slice | solution.py:200
  263.3 5.5 %dynamic_update_slice.48 = f32[3,12,12,132]{3,2,1,0:T(8,128)S(1)} dynamic-update-slice(f32[3,12,12,132]{3,2,1,0:T(8,128)S(1)} %dynamic_update_slice.47, f32[3,12,12,12]{3,2,1,0:T(8,128)S(1)} %convolution_add_fusion.9, s32[]{:T(128)} %constant.666.clone.1..sunk, s32[]{:T(128)} %constant.666.clone.1..sunk, s32[]{:T(128)} %constant.666.clone.1..sunk, s32[]{:T(128)S(6)} %select_n.1307) | dynamic-update-slice | bytes 41476 | tf_op jit(solution)/shard_map/while/body/eval_jaxpr/dynamic_update_slice | solution.py:200
  269.3 5.5 %dynamic_update_slice.49 = f32[3,12,12,132]{3,2,1,0:T(8,128)S(1)} dynamic-update-slice(f32[3,12,12,132]{3,2,1,0:T(8,128)S(1)} %dynamic_update_slice.48, f32[3,12,12,12]{3,2,1,0:T(8,128)S(1)} %convolution_add_fusion.10, s32[]{:T(128)} %constant.666.clone.1..sunk, s32[]{:T(128)} %constant.666.clone.1..sunk, s32[]{:T(128)} %constant.666.clone.1..sunk, s32[]{:T(128)S(6)} %select_n.1333) | dynamic-update-slice | bytes 41476 | tf_op jit(solution)/shard_map/while/body/eval_jaxpr/dynamic_update_slice | solution.py:200
  275.4 5.5 %dynamic_update_slice.50 = f32[3,12,12,132]{3,2,1,0:T(8,128)S(1)} dynamic-update-slice(f32[3,12,12,132]{3,2,1,0:T(8,128)S(1)} %dynamic_update_slice.49, f32[3,12,12,12]{3,2,1,0:T(8,128)S(1)} %convolution_add_fusion.11, s32[]{:T(128)} %constant.666.clone.1..sunk, s32[]{:T(128)} %constant.666.clone.1..sunk, s32[]{:T(128)} %constant.666.clone.1..sunk, s32[]{:T(128)S(6)} %select_n.1332) | dynamic-update-slice | bytes 41476 | tf_op jit(solution)/shard_map/while/body/eval_jaxpr/dynamic_update_slice | solution.py:200
  281.4 1.9 collective-permute-start.18
  283.3 4.6 %collective-permute-start.19 = (f32[3,12,12,2]{3,2,1,0:T(8,128)S(1)}, f32[3,12,12,2]{3,2,1,0:T(8,128)S(1)}, u32[]{:S(2)}, u32[]{:S(2)}) collective-permute-start(f32[3,12,12,2]{3,2,1,0:T(8,128)S(1)} %get-tuple-element.392), channel_id=1, source_target_pairs={{32,0},{64,32},{96,64},{128,96},{160,128},{192,160},{224,192},{256... | collective-permute-start | bytes 10376 | tf_op jit(solution)/shard_map/ppermute | solution.py:53
  287.9 1.0 scatter_fusion
  288.9 1.9 collective-permute-start.24
  290.9 4.6 %collective-permute-start.25 = (f32[6,3,3,1,2,128]{5,0,4,3,2,1:T(8,128)S(1)}, f32[6,3,3,1,2,128]{5,0,4,3,2,1:T(8,128)S(1)}, u32[]{:S(2)}, u32[]{:S(2)}) collective-permute-start(f32[6,3,3,1,2,128]{5,0,4,3,2,1:T(8,128)S(1)} %get-tuple-element.402), channel_id=1, source_target_pairs={{32,0},{64,32},{96,64},{128,96},{160,128},{192,160},{224,192},{256... | collective-permute-start | bytes 165896 | tf_op jit(solution)/shard_map/ppermute | solution.py:53
  295.8 2.9 collective-permute-start.20
  299.1 1.1 collective-permute-done.20
  300.1 2.7 collective-permute-done.21
  303.0 3.5 %collective-permute-start.22 = (f32[3,2,16,136]{3,2,1,0:T(8,128)S(1)}, f32[3,2,16,136]{3,2,1,0:T(8,128)S(1)}, u32[]{:S(2)}, u32[]{:S(2)}) collective-permute-start(f32[3,2,16,136]{3,2,1,0:T(8,128)S(1)} %get-tuple-element.381), channel_id=1, source_target_pairs={{0,1},{1,2},{2,3},{3,0},{4,5},{5,6},{6,7},{7,4},{8,9},{9,10},{10,1... | collective-permute-start | bytes 156680 | tf_op jit(solution)/shard_map/ppermute | solution.py:51
  306.5 3.4 %collective-permute-start.23 = (f32[3,2,16,136]{3,2,1,0:T(8,128)S(1)}, f32[3,2,16,136]{3,2,1,0:T(8,128)S(1)}, u32[]{:S(2)}, u32[]{:S(2)}) collective-permute-start(f32[3,2,16,136]{3,2,1,0:T(8,128)S(1)} %get-tuple-element.382), channel_id=1, source_target_pairs={{1,0},{2,1},{3,2},{0,3},{5,4},{6,5},{7,6},{4,7},{9,8},{10,9},{11,1... | collective-permute-start | bytes 156680 | tf_op jit(solution)/shard_map/ppermute | solution.py:53
  310.6 1.0 collective-permute-start.27
  312.5 2.4 collective-permute-done.27
  315.0 2.1 collective-permute-start.28
  317.1 4.4 %collective-permute-start.29 = (f32[6,1,5,5,2,128]{5,0,4,3,2,1:T(8,128)S(1)}, f32[6,1,5,5,2,128]{5,0,4,3,2,1:T(8,128)S(1)}, u32[]{:S(2)}, u32[]{:S(2)}) collective-permute-start(f32[6,1,5,5,2,128]{5,0,4,3,2,1:T(8,128)S(1)} %get-tuple-element.390), channel_id=1, source_target_pairs={{1,0},{2,1},{3,2},{0,3},{5,4},{6,5},{7,6},{4,7},{9,8},{10,9},{11,1... | collective-permute-start | bytes 460808 | tf_op jit(solution)/shard_map/ppermute | solution.py:53
  322.7 1.5 collective-permute-done.29
  (266 shorter events, 53.3 us)
Async XLA Ops:
  0.6 10.0 %copy-start = (bf16[19,8,8,128]{3,2,1,0:T(8,128)(2,1)S(1)}, bf16[19,8,8,128]{3,2,1,0:T(8,128)(2,1)}, u32[]{:S(2)}) copy-start(bf16[19,8,8,128]{3,2,1,0:T(8,128)(2,1)} %param.11) | copy-start | bytes 933892
  8.2 30.4 %copy-start.5 = (s32[16]{0:T(128)S(1)}, s32[16]{0:T(128)}, u32[]{:S(2)}) copy-start(s32[16]{0:T(128)} %param.16) | copy-start | bytes 196
  16.2 27.9 %copy-start.7 = (s32[16]{0:T(128)S(1)}, s32[16]{0:T(128)}, u32[]{:S(2)}) copy-start(s32[16]{0:T(128)} %param.17) | copy-start | bytes 196
  16.9 21.8 %collective-permute-start = (f32[19,8,8,1]{0,2,3,1:T(8,128)S(1)}, f32[19,8,8,1]{0,2,3,1:T(8,128)S(1)}, u32[]{:S(2)}, u32[]{:S(2)}) collective-permute-start(f32[19,8,8,1]{0,2,3,1:T(8,128)S(1)} %copy.119), channel_id=1, source_target_pairs={{0,32},{32,64},{64,96},{96,128},{128,160},{160,192},{192,224},{224... | collective-permute-start | bytes 14600 | tf_op jit(solution)/shard_map/ppermute | solution.py:51
  21.8 17.8 %collective-permute-start.1 = (f32[19,8,8,1]{0,2,3,1:T(8,128)S(1)}, f32[19,8,8,1]{0,2,3,1:T(8,128)S(1)}, u32[]{:S(2)}, u32[]{:S(2)}) collective-permute-start(f32[19,8,8,1]{0,2,3,1:T(8,128)S(1)} %copy.120), channel_id=1, source_target_pairs={{32,0},{64,32},{96,64},{128,96},{160,128},{192,160},{224,192},{256... | collective-permute-start | bytes 14600 | tf_op jit(solution)/shard_map/ppermute | solution.py:53
  41.4 4.8 %collective-permute-start.2 = (f32[19,8,1,130]{3,2,1,0:T(1,128)S(1)}, f32[19,8,1,130]{3,2,1,0:T(1,128)S(1)}, u32[]{:S(2)}, u32[]{:S(2)}) collective-permute-start(f32[19,8,1,130]{3,2,1,0:T(1,128)S(1)} %get-tuple-element.379), channel_id=1, source_target_pairs={{0,4},{4,8},{8,12},{12,16},{16,20},{20,24},{24,28},{28,0},{1,5},{5... | collective-permute-start | bytes 237128 | tf_op jit(solution)/shard_map/ppermute | solution.py:51
  44.0 4.7 %collective-permute-start.3 = (f32[19,8,1,130]{3,2,1,0:T(1,128)S(1)}, f32[19,8,1,130]{3,2,1,0:T(1,128)S(1)}, u32[]{:S(2)}, u32[]{:S(2)}) collective-permute-start(f32[19,8,1,130]{3,2,1,0:T(1,128)S(1)} %get-tuple-element.380), channel_id=1, source_target_pairs={{4,0},{8,4},{12,8},{16,12},{20,16},{24,20},{28,24},{0,28},{5,1},{9... | collective-permute-start | bytes 237128 | tf_op jit(solution)/shard_map/ppermute | solution.py:53
  49.0 12.0 %collective-permute-start.4 = (f32[19,1,10,130]{3,2,1,0:T(8,128)S(1)}, f32[19,1,10,130]{3,2,1,0:T(8,128)S(1)}, u32[]{:S(2)}, u32[]{:S(2)}) collective-permute-start(f32[19,1,10,130]{3,2,1,0:T(8,128)S(1)} %get-tuple-element.375), channel_id=1, source_target_pairs={{0,1},{1,2},{2,3},{3,0},{4,5},{5,6},{6,7},{7,4},{8,9},{9,10},{10,1... | collective-permute-start | bytes 296408 | tf_op jit(solution)/shard_map/ppermute | solution.py:51
  52.2 10.4 %collective-permute-start.5 = (f32[19,1,10,130]{3,2,1,0:T(8,128)S(1)}, f32[19,1,10,130]{3,2,1,0:T(8,128)S(1)}, u32[]{:S(2)}, u32[]{:S(2)}) collective-permute-start(f32[19,1,10,130]{3,2,1,0:T(8,128)S(1)} %get-tuple-element.376), channel_id=1, source_target_pairs={{1,0},{2,1},{3,2},{0,3},{5,4},{6,5},{7,6},{4,7},{9,8},{10,9},{11,1... | collective-permute-start | bytes 296408 | tf_op jit(solution)/shard_map/ppermute | solution.py:53
  65.5 13.7 %copy-start.1 = (f32[3,16,128]{2,1,0:T(8,128)S(1)}, f32[3,16,128]{2,1,0:T(8,128)}, u32[]{:S(2)}) copy-start(f32[3,16,128]{2,1,0:T(8,128)} %param.13) | copy-start | bytes 73732
  65.5 13.7 %copy-start.2 = (f32[3,16,128]{2,1,0:T(8,128)S(1)}, f32[3,16,128]{2,1,0:T(8,128)}, u32[]{:S(2)}) copy-start(f32[3,16,128]{2,1,0:T(8,128)} %param.14) | copy-start | bytes 73732
  66.3 7.6 %collective-permute-start.6 = (f32[19,8,8,1]{0,2,3,1:T(8,128)S(1)}, f32[19,8,8,1]{0,2,3,1:T(8,128)S(1)}, u32[]{:S(2)}, u32[]{:S(2)}) collective-permute-start(f32[19,8,8,1]{0,2,3,1:T(8,128)S(1)} %copy.123), channel_id=1, source_target_pairs={{0,32},{32,64},{64,96},{96,128},{128,160},{160,192},{192,224},{224... | collective-permute-start | bytes 14600 | tf_op jit(solution)/shard_map/ppermute | solution.py:51
  68.8 6.2 %collective-permute-start.7 = (f32[19,8,8,1]{0,2,3,1:T(8,128)S(1)}, f32[19,8,8,1]{0,2,3,1:T(8,128)S(1)}, u32[]{:S(2)}, u32[]{:S(2)}) collective-permute-start(f32[19,8,8,1]{0,2,3,1:T(8,128)S(1)} %copy.124), channel_id=1, source_target_pairs={{32,0},{64,32},{96,64},{128,96},{160,128},{192,160},{224,192},{256... | collective-permute-start | bytes 14600 | tf_op jit(solution)/shard_map/ppermute | solution.py:53
  76.7 4.7 %collective-permute-start.8 = (f32[19,8,1,130]{3,2,1,0:T(1,128)S(1)}, f32[19,8,1,130]{3,2,1,0:T(1,128)S(1)}, u32[]{:S(2)}, u32[]{:S(2)}) collective-permute-start(f32[19,8,1,130]{3,2,1,0:T(1,128)S(1)} %get-tuple-element.377), channel_id=1, source_target_pairs={{0,4},{4,8},{8,12},{12,16},{16,20},{20,24},{24,28},{28,0},{1,5},{5... | collective-permute-start | bytes 237128 | tf_op jit(solution)/shard_map/ppermute | solution.py:51
  79.2 5.0 %collective-permute-start.9 = (f32[19,8,1,130]{3,2,1,0:T(1,128)S(1)}, f32[19,8,1,130]{3,2,1,0:T(1,128)S(1)}, u32[]{:S(2)}, u32[]{:S(2)}) collective-permute-start(f32[19,8,1,130]{3,2,1,0:T(1,128)S(1)} %get-tuple-element.378), channel_id=1, source_target_pairs={{4,0},{8,4},{12,8},{16,12},{20,16},{24,20},{28,24},{0,28},{5,1},{9... | collective-permute-start | bytes 237128 | tf_op jit(solution)/shard_map/ppermute | solution.py:53
  84.5 11.5 %collective-permute-start.10 = (f32[19,1,10,130]{3,2,1,0:T(8,128)S(1)}, f32[19,1,10,130]{3,2,1,0:T(8,128)S(1)}, u32[]{:S(2)}, u32[]{:S(2)}) collective-permute-start(f32[19,1,10,130]{3,2,1,0:T(8,128)S(1)} %get-tuple-element.373), channel_id=1, source_target_pairs={{0,1},{1,2},{2,3},{3,0},{4,5},{5,6},{6,7},{7,4},{8,9},{9,10},{10,1... | collective-permute-start | bytes 296408 | tf_op jit(solution)/shard_map/ppermute | solution.py:51
  87.7 10.0 %collective-permute-start.11 = (f32[19,1,10,130]{3,2,1,0:T(8,128)S(1)}, f32[19,1,10,130]{3,2,1,0:T(8,128)S(1)}, u32[]{:S(2)}, u32[]{:S(2)}) collective-permute-start(f32[19,1,10,130]{3,2,1,0:T(8,128)S(1)} %get-tuple-element.374), channel_id=1, source_target_pairs={{1,0},{2,1},{3,2},{0,3},{5,4},{6,5},{7,6},{4,7},{9,8},{10,9},{11,1... | collective-permute-start | bytes 296408 | tf_op jit(solution)/shard_map/ppermute | solution.py:53
  99.9 7.6 %collective-permute-start.12 = (f32[3,8,8,2]{3,2,1,0:T(8,128)S(1)}, f32[3,8,8,2]{3,2,1,0:T(8,128)S(1)}, u32[]{:S(2)}, u32[]{:S(2)}) collective-permute-start(f32[3,8,8,2]{3,2,1,0:T(8,128)S(1)} %get-tuple-element.405), channel_id=1, source_target_pairs={{0,32},{32,64},{64,96},{96,128},{128,160},{160,192},{192,224},{224... | collective-permute-start | bytes 4616 | tf_op jit(solution)/shard_map/ppermute | solution.py:51
  101.8 6.8 %collective-permute-start.13 = (f32[3,8,8,2]{3,2,1,0:T(8,128)S(1)}, f32[3,8,8,2]{3,2,1,0:T(8,128)S(1)}, u32[]{:S(2)}, u32[]{:S(2)}) collective-permute-start(f32[3,8,8,2]{3,2,1,0:T(8,128)S(1)} %get-tuple-element.406), channel_id=1, source_target_pairs={{32,0},{64,32},{96,64},{128,96},{160,128},{192,160},{224,192},{256... | collective-permute-start | bytes 4616 | tf_op jit(solution)/shard_map/ppermute | solution.py:53
  108.8 4.0 %collective-permute-start.14 = (f32[3,8,2,132]{3,2,1,0:T(2,128)S(1)}, f32[3,8,2,132]{3,2,1,0:T(2,128)S(1)}, u32[]{:S(2)}, u32[]{:S(2)}) collective-permute-start(f32[3,8,2,132]{3,2,1,0:T(2,128)S(1)} %get-tuple-element.397), channel_id=1, source_target_pairs={{0,4},{4,8},{8,12},{12,16},{16,20},{20,24},{24,28},{28,0},{1,5},{5... | collective-permute-start | bytes 76040 | tf_op jit(solution)/shard_map/ppermute | solution.py:51
  111.6 3.8 %collective-permute-start.15 = (f32[3,8,2,132]{3,2,1,0:T(2,128)S(1)}, f32[3,8,2,132]{3,2,1,0:T(2,128)S(1)}, u32[]{:S(2)}, u32[]{:S(2)}) collective-permute-start(f32[3,8,2,132]{3,2,1,0:T(2,128)S(1)} %get-tuple-element.398), channel_id=1, source_target_pairs={{4,0},{8,4},{12,8},{16,12},{20,16},{24,20},{28,24},{0,28},{5,1},{9... | collective-permute-start | bytes 76040 | tf_op jit(solution)/shard_map/ppermute | solution.py:53
  115.6 6.6 %collective-permute-start.16 = (f32[3,2,12,132]{3,2,1,0:T(8,128)S(1)}, f32[3,2,12,132]{3,2,1,0:T(8,128)S(1)}, u32[]{:S(2)}, u32[]{:S(2)}) collective-permute-start(f32[3,2,12,132]{3,2,1,0:T(8,128)S(1)} %get-tuple-element.393), channel_id=1, source_target_pairs={{0,1},{1,2},{2,3},{3,0},{4,5},{5,6},{6,7},{7,4},{8,9},{9,10},{10,1... | collective-permute-start | bytes 114056 | tf_op jit(solution)/shard_map/ppermute | solution.py:51
  118.5 5.4 %collective-permute-start.17 = (f32[3,2,12,132]{3,2,1,0:T(8,128)S(1)}, f32[3,2,12,132]{3,2,1,0:T(8,128)S(1)}, u32[]{:S(2)}, u32[]{:S(2)}) collective-permute-start(f32[3,2,12,132]{3,2,1,0:T(8,128)S(1)} %get-tuple-element.394), channel_id=1, source_target_pairs={{1,0},{2,1},{3,2},{0,3},{5,4},{6,5},{7,6},{4,7},{9,8},{10,9},{11,1... | collective-permute-start | bytes 114056 | tf_op jit(solution)/shard_map/ppermute | solution.py:53
  122.1 2.0 copy-start.3
  281.4 14.1 %collective-permute-start.18 = (f32[3,12,12,2]{3,2,1,0:T(8,128)S(1)}, f32[3,12,12,2]{3,2,1,0:T(8,128)S(1)}, u32[]{:S(2)}, u32[]{:S(2)}) collective-permute-start(f32[3,12,12,2]{3,2,1,0:T(8,128)S(1)} %get-tuple-element.391), channel_id=1, source_target_pairs={{0,32},{32,64},{64,96},{96,128},{128,160},{160,192},{192,224},{224... | collective-permute-start | bytes 10376 | tf_op jit(solution)/shard_map/ppermute | solution.py:51
  283.3 12.2 %collective-permute-start.19 = (f32[3,12,12,2]{3,2,1,0:T(8,128)S(1)}, f32[3,12,12,2]{3,2,1,0:T(8,128)S(1)}, u32[]{:S(2)}, u32[]{:S(2)}) collective-permute-start(f32[3,12,12,2]{3,2,1,0:T(8,128)S(1)} %get-tuple-element.392), channel_id=1, source_target_pairs={{32,0},{64,32},{96,64},{128,96},{160,128},{192,160},{224,192},{256... | collective-permute-start | bytes 10376 | tf_op jit(solution)/shard_map/ppermute | solution.py:53
  288.9 21.4 %collective-permute-start.24 = (f32[6,3,3,1,2,128]{5,0,4,3,2,1:T(8,128)S(1)}, f32[6,3,3,1,2,128]{5,0,4,3,2,1:T(8,128)S(1)}, u32[]{:S(2)}, u32[]{:S(2)}) collective-permute-start(f32[6,3,3,1,2,128]{5,0,4,3,2,1:T(8,128)S(1)} %get-tuple-element.401), channel_id=1, source_target_pairs={{0,32},{32,64},{64,96},{96,128},{128,160},{160,192},{192,224},{224... | collective-permute-start | bytes 165896 | tf_op jit(solution)/shard_map/ppermute | solution.py:51
  290.9 21.1 %copy-start.6 = (pred[8]{0:T(512)(128)(4,1)S(1)}, pred[8]{0:T(512)(128)(4,1)}, u32[]{:S(2)}) copy-start(pred[8]{0:T(512)(128)(4,1)} %constant.672.clone.1) | copy-start | bytes 28
  290.9 19.4 %collective-permute-start.25 = (f32[6,3,3,1,2,128]{5,0,4,3,2,1:T(8,128)S(1)}, f32[6,3,3,1,2,128]{5,0,4,3,2,1:T(8,128)S(1)}, u32[]{:S(2)}, u32[]{:S(2)}) collective-permute-start(f32[6,3,3,1,2,128]{5,0,4,3,2,1:T(8,128)S(1)} %get-tuple-element.402), channel_id=1, source_target_pairs={{32,0},{64,32},{96,64},{128,96},{160,128},{192,160},{224,192},{256... | collective-permute-start | bytes 165896 | tf_op jit(solution)/shard_map/ppermute | solution.py:53
  295.8 4.3 %collective-permute-start.20 = (f32[3,12,2,136]{3,2,1,0:T(2,128)S(1)}, f32[3,12,2,136]{3,2,1,0:T(2,128)S(1)}, u32[]{:S(2)}, u32[]{:S(2)}) collective-permute-start(f32[3,12,2,136]{3,2,1,0:T(2,128)S(1)} %get-tuple-element.383), channel_id=1, source_target_pairs={{0,4},{4,8},{8,12},{12,16},{16,20},{20,24},{24,28},{28,0},{1,5},{5... | collective-permute-start | bytes 117512 | tf_op jit(solution)/shard_map/ppermute | solution.py:51
  298.7 4.1 %collective-permute-start.21 = (f32[3,12,2,136]{3,2,1,0:T(2,128)S(1)}, f32[3,12,2,136]{3,2,1,0:T(2,128)S(1)}, u32[]{:S(2)}, u32[]{:S(2)}) collective-permute-start(f32[3,12,2,136]{3,2,1,0:T(2,128)S(1)} %get-tuple-element.384), channel_id=1, source_target_pairs={{4,0},{8,4},{12,8},{16,12},{20,16},{24,20},{28,24},{0,28},{5,1},{9... | collective-permute-start | bytes 117512 | tf_op jit(solution)/shard_map/ppermute | solution.py:53
  302.9 18.6 %copy-start.4 = (pred[128]{0:T(512)(128)(4,1)S(1)}, pred[128]{0:T(512)(128)(4,1)}, u32[]{:S(2)}) copy-start(pred[128]{0:T(512)(128)(4,1)} %constant.673.clone.1) | copy-start | bytes 388
  303.0 8.7 %collective-permute-start.22 = (f32[3,2,16,136]{3,2,1,0:T(8,128)S(1)}, f32[3,2,16,136]{3,2,1,0:T(8,128)S(1)}, u32[]{:S(2)}, u32[]{:S(2)}) collective-permute-start(f32[3,2,16,136]{3,2,1,0:T(8,128)S(1)} %get-tuple-element.381), channel_id=1, source_target_pairs={{0,1},{1,2},{2,3},{3,0},{4,5},{5,6},{6,7},{7,4},{8,9},{9,10},{10,1... | collective-permute-start | bytes 156680 | tf_op jit(solution)/shard_map/ppermute | solution.py:51
  306.5 5.4 %collective-permute-start.23 = (f32[3,2,16,136]{3,2,1,0:T(8,128)S(1)}, f32[3,2,16,136]{3,2,1,0:T(8,128)S(1)}, u32[]{:S(2)}, u32[]{:S(2)}) collective-permute-start(f32[3,2,16,136]{3,2,1,0:T(8,128)S(1)} %get-tuple-element.382), channel_id=1, source_target_pairs={{1,0},{2,1},{3,2},{0,3},{5,4},{6,5},{7,6},{4,7},{9,8},{10,9},{11,1... | collective-permute-start | bytes 156680 | tf_op jit(solution)/shard_map/ppermute | solution.py:53
  310.4 2.2 collective-permute-start.26
  310.6 4.3 %collective-permute-start.27 = (f32[6,3,1,5,2,128]{5,0,4,3,2,1:T(8,128)S(1)}, f32[6,3,1,5,2,128]{5,0,4,3,2,1:T(8,128)S(1)}, u32[]{:S(2)}, u32[]{:S(2)}) collective-permute-start(f32[6,3,1,5,2,128]{5,0,4,3,2,1:T(8,128)S(1)} %get-tuple-element.396), channel_id=1, source_target_pairs={{4,0},{8,4},{12,8},{16,12},{20,16},{24,20},{28,24},{0,28},{5,1},{9... | collective-permute-start | bytes 276488 | tf_op jit(solution)/shard_map/ppermute | solution.py:53
  315.0 7.7 %collective-permute-start.28 = (f32[6,1,5,5,2,128]{5,0,4,3,2,1:T(8,128)S(1)}, f32[6,1,5,5,2,128]{5,0,4,3,2,1:T(8,128)S(1)}, u32[]{:S(2)}, u32[]{:S(2)}) collective-permute-start(f32[6,1,5,5,2,128]{5,0,4,3,2,1:T(8,128)S(1)} %get-tuple-element.389), channel_id=1, source_target_pairs={{0,1},{1,2},{2,3},{3,0},{4,5},{5,6},{6,7},{7,4},{8,9},{9,10},{10,1... | collective-permute-start | bytes 460808 | tf_op jit(solution)/shard_map/ppermute | solution.py:51
  317.1 7.1 %collective-permute-start.29 = (f32[6,1,5,5,2,128]{5,0,4,3,2,1:T(8,128)S(1)}, f32[6,1,5,5,2,128]{5,0,4,3,2,1:T(8,128)S(1)}, u32[]{:S(2)}, u32[]{:S(2)}) collective-permute-start(f32[6,1,5,5,2,128]{5,0,4,3,2,1:T(8,128)S(1)} %get-tuple-element.390), channel_id=1, source_target_pairs={{1,0},{2,1},{3,2},{0,3},{5,4},{6,5},{7,6},{4,7},{9,8},{10,9},{11,1... | collective-permute-start | bytes 460808 | tf_op jit(solution)/shard_map/ppermute | solution.py:53
where the time goes:
time: 330 us; the launch traced here: 325 us
  local copies, waits for them, and re-layouts  103 us (31%)
  starting transfers between devices  93.9 us (28%)
  loops' own time  44.4 us (13%)
  waiting for transfers between devices  38.6 us (12%)
  other arithmetic  27.8 us (8%)
  matrix products  16.3 us (5%)
    dynamic_update_slice x16, local copies, waits for them, and re-layouts, droplet_group(): lax.dynamic_update_slice(spread, lax.dynamic_slice(spread, corner, (3, ed...  88.7 us
    ppermute x15, starting transfers between devices, with_halo(): lax.ppermute(head, axis, [((i + 1) % count, i) for i in range(count)])  55.7 us
    another operation x1, loops' own time, local(): lax.scan(droplet_group, jnp.zeros_like(velocity_ext), (homes, speeds, fra...  44.4 us
    ppermute x15, starting transfers between devices, with_halo(): lax.ppermute(tail, axis, [(i, (i + 1) % count) for i in range(count)])  38.2 us
    ppermute x15, waiting for transfers between devices, with_halo(): lax.ppermute(head, axis, [((i + 1) % count, i) for i in range(count)])  21.1 us
    ppermute x15, waiting for transfers between devices, with_halo(): lax.ppermute(tail, axis, [(i, (i + 1) % count) for i in range(count)])  17.4 us
    unnamed x36, other arithmetic  15.7 us
    dot_general x16, matrix products, droplet_group(): jnp.dot(tile.reshape(3 * edge * edge, edge), weight_x.T, precision=highest)  8.3 us
  transfers between devices with their start and end apart: 30, of which 21 were waited for; matrix products, arithmetic and copies ran while one was open for 2% of the time, Pallas kernels for 0%

commit v1 on v0

v1 whole, which is shorter than its diff:
```python
import math

import jax
import jax.numpy as jnp
import numpy as np
from jax import lax
from jax.experimental import pallas as pl
from jax.experimental.pallas import tpu as pltpu
from jax.sharding import PartitionSpec as P

lattice = [
    (0, 0, 0), (1, 0, 0), (-1, 0, 0), (0, 1, 0), (0, -1, 0), (0, 0, 1), (0, 0, -1),
    (1, 1, 0), (-1, -1, 0), (1, -1, 0), (-1, 1, 0), (1, 0, 1), (-1, 0, -1), (1, 0, -1),
    (-1, 0, 1), (0, 1, 1), (0, -1, -1), (0, 1, -1), (0, -1, 1),
]
weights_table = [1.0 / 3.0] + [1.0 / 18.0] * 6 + [1.0 / 36.0] * 12
opposite = [0, 2, 1, 4, 3, 6, 5, 8, 7, 10, 9, 12, 11, 14, 13, 16, 15, 18, 17]
inverse_tau = 0.8
relax = 0.5
couple = 8.0
f32 = jnp.float32
bf16 = jnp.bfloat16

face_pops = {}
for axis in range(3):
    for sign in (1, -1):
        d = [0, 0, 0]
        d[axis] = sign
        face_pops[tuple(d)] = [i for i in range(19) if lattice[i][axis] == sign]
post_msgs = {}
tiles = 0
for i in range(1, 19):
    c = lattice[i]
    count = 1 if (abs(c[0]) + abs(c[1]) + abs(c[2]) > 1 or c[0] != 0) else 5
    post_msgs[c] = (tiles, count)
    tiles += count
POST_TILES = tiles

regions = {
    (0, 0): (0, 24),
    (-1, 0): (24, 6),
    (1, 0): (30, 3),
    (0, -1): (33, 6),
    (0, 1): (39, 3),
    (-1, -1): (42, 2),
    (1, -1): (44, 1),
    (-1, 1): (45, 1),
    (1, 1): (46, 1),
}
region_list = list(regions)
ROWS = 48 * 8
all_dirs = [(x, y, z) for z in (-1, 0, 1) for y in (-1, 0, 1) for x in (-1, 0, 1) if (x, y, z) != (0, 0, 0)]
N_POST = 18
N_MSG = 2 * N_POST + 3 * 26
PAIRS = 8
BLOCKS = 16


def corner_rows(region):
    dy, dz = region
    ys = [7] if dy == 1 else [0, 1]
    zs = [7] if dz == 1 else [0, 1]
    return [(c, y, z) for c in range(3) for z in zs for y in ys]


def tile_rows(t):
    return pl.ds(t * 8, 8)


def kernel(
    sizes,
    pops, coarse, interface, drop_vel, drop_frac, home, counts, dest,
    state_hbm, force, arrived,
    posts, state, psend, precv, vmain, vhalo, vsend, pksend, pkrecv, vhi, vlo, whi, wlo,
    taps, homes, shi, slo, facc, fsend, frecv, fpsend, fprecv, states, outbox, inbox,
    send_sem, recv_sem, out_sem,
):
    n_x, n_y, n_z = sizes
    me = (lax.axis_index("gx"), lax.axis_index("gy"), lax.axis_index("gz"))
    level = me[2]
    at_bottom = level == 0
    at_top = level == n_z - 1

    def moved_by(axis, step, size):
        if step == 0:
            return me[axis]
        return lax.rem(me[axis] + (step + size), size)

    coords = {
        (axis, step): moved_by(axis, step, size)
        for axis, size in enumerate(sizes)
        for step in (-1, 0, 1)
    }

    def device(d):
        return {"gx": coords[0, d[0]], "gy": coords[1, d[1]], "gz": coords[2, d[2]]}

    lane = lax.broadcasted_iota(jnp.int32, (8, 128), 1)
    sub = lax.broadcasted_iota(jnp.int32, (8, 128), 0)

    started = []

    def copy(index, src, dst, d):
        made = pltpu.make_async_remote_copy(
            src_ref=src,
            dst_ref=dst,
            send_sem=send_sem.at[index],
            recv_sem=recv_sem.at[index],
            device_id=device(d),
            device_id_type=pl.DeviceIdType.MESH,
        )
        made.start()
        started.append(made)
        return made

    barrier = pltpu.get_barrier_semaphore()
    for d in all_dirs:
        pl.semaphore_signal(barrier, inc=1, device_id=device(d), device_id_type=pl.DeviceIdType.MESH)

    def macroscopic(values):
        density = values[0] * weights_table[0]
        moment = [None, None, None]
        for index in range(1, 19):
            term = values[index] * weights_table[index]
            density = density + term
            for axis in range(3):
                sign = lattice[index][axis]
                if sign == 1:
                    moment[axis] = term if moment[axis] is None else moment[axis] + term
                if sign == -1:
                    moment[axis] = moment[axis] - term
        inverse = 1.0 / density
        return density, [m * inverse for m in moment]

    def collide(source):
        @pl.loop(0, 8)
        def _(z):
            rows = pl.ds(pl.multiple_of(z * 8, 8), 8)
            values = [source[i, rows, :] for i in range(19)]
            density, flow = macroscopic(values)
            square = flow[0] * flow[0] + flow[1] * flow[1] + flow[2] * flow[2]
            inside = interface[z] == 1
            base = 1.0 - 1.5 * square
            for i in range(19):
                along = None
                for axis in range(3):
                    sign = lattice[i][axis]
                    if sign == 1:
                        along = flow[axis] if along is None else along + flow[axis]
                    if sign == -1:
                        along = -flow[axis] if along is None else along - flow[axis]
                if along is None:
                    balance = density * base
                else:
                    balance = density * (base + along * (3.0 + 4.5 * along))
                relaxed = values[i] - (values[i] - balance) * inverse_tau
                posts[i, rows, :] = jnp.where(inside, coarse[i, z].astype(f32), relaxed)

    def send_posts(r):
        copies = {}
        for number, (d, (first, count)) in enumerate(post_msgs.items()):
            layer = {a: (7 if d[a] == 1 else 0) for a in (1, 2)}
            if d in face_pops:
                listed = face_pops[d]
            else:
                listed = [lattice.index(d)]
            if d[0] != 0 and d[1] == 0 and d[2] == 0:
                acc = jnp.zeros((8, 128), f32)
                from_lane = 127 if d[0] == 1 else 0
                for k, i in enumerate(listed):
                    for z in range(8):
                        spot = k * 8 + z
                        turned = pltpu.roll(posts[i, tile_rows(z), :], (spot - from_lane) % 128, 1)
                        acc = jnp.where(lane == spot, turned, acc)
                psend[r, tile_rows(first), :] = acc
            elif d[2] != 0:
                for k, i in enumerate(listed):
                    psend[r, tile_rows(first + k), :] = posts[i, tile_rows(layer[2]), :]
            else:
                for k, i in enumerate(listed):
                    psend[r, tile_rows(first + k), :] = posts[i, pl.ds(layer[1], 8, stride=8), :]
            part = pl.ds(first * 8, count * 8)
            copies[d] = copy(r * N_POST + number, psend.at[r, part], precv.at[r, part], d)
        return copies

    def pull(r, i):
        cx, cy, cz = lattice[i]
        far = 127 if cx == 1 else 0

        def halo(d):
            first, count = post_msgs[d]
            k = face_pops[d].index(i) if d in face_pops and d[0] == 0 else 0
            return first + k

        def x_shift(value, beyond):
            return pltpu.roll(jnp.where(lane == far, beyond, value), cx % 128, 1)

        def y_shift(value, row):
            edge = 0 if cy == 1 else 7
            return jnp.where(sub == edge, row, pltpu.roll(value, cy % 8, 0))

        wanted = [z - cz for z in range(8)]
        planes = {z: posts[i, tile_rows(z), :] for z in range(8) if z in wanted}
        outer = None
        if cz != 0:
            outer = precv[r, tile_rows(halo((0, 0, cz))), :]
        if cx != 0:
            packed = precv[r, tile_rows(post_msgs[(cx, 0, 0)][0]), :]
            k = face_pops[(cx, 0, 0)].index(i)
            for z in planes:
                planes[z] = x_shift(planes[z], pltpu.roll(packed, (far - (k * 8 + z)) % 128, 1))
            if cz != 0:
                outer = x_shift(outer, precv[r, tile_rows(halo((cx, 0, cz))), :])
        if cy != 0:
            place = halo((0, cy, 0))
            if cx != 0:
                side = x_shift(precv[r, tile_rows(place), :], precv[r, tile_rows(halo((cx, cy, 0))), :])
                for z in planes:
                    planes[z] = y_shift(planes[z], side[z : z + 1, :])
            else:
                for z in planes:
                    planes[z] = y_shift(planes[z], precv[r, pl.ds(place * 8 + z, 1), :])
            if cz != 0:
                row = halo((0, cy, cz)) * 8 + (7 if cy == 1 else 0)
                outer = y_shift(outer, precv[r, pl.ds(row, 1), :])
        out = [planes[z] if z in planes else outer for z in wanted]
        if cz == 1:
            out[0] = jnp.where(at_bottom, posts[opposite[i], tile_rows(0), :], out[0])
        if cz == -1:
            out[7] = jnp.where(at_top, posts[opposite[i], tile_rows(7), :], out[7])
        return out

    def stream(r, copies):
        for made in copies.values():
            made.wait_recv()
        for i in range(19):
            out = pull(r, i)
            for z in range(8):
                state[r, i, tile_rows(z), :] = out[z]

    def prepare():
        for axis in range(3):
            angle = drop_frac[axis] * (0.5 * math.pi)
            sine = jnp.sin(angle)
            cosine = jnp.cos(angle)
            taps[axis * 4 + 0] = 0.25 - 0.25 * sine
            taps[axis * 4 + 1] = 0.25 + 0.25 * cosine
            taps[axis * 4 + 2] = 0.25 + 0.25 * sine
            taps[axis * 4 + 3] = 0.25 - 0.25 * cosine
        cells = home[...]
        homes[0] = (cells & 127) - 1
        homes[1] = ((cells >> 7) & 7) - 1
        homes[2] = (cells >> 10) - 1

    def picked(offset, weight):
        zero = jnp.zeros(offset.shape, f32)
        return jnp.where(
            offset == 0,
            weight[0],
            jnp.where(offset == 1, weight[1], jnp.where(offset == 2, weight[2], jnp.where(offset == 3, weight[3], zero))),
        )

    def build_weights(low, high):
        rows16 = lax.broadcasted_iota(jnp.int32, (16, 128), 0)

        @pl.loop(low, high)
        def _(p):
            for j in range(2):
                block = pl.ds(2 * p + j, 1)
                lanes = pl.ds(j * 128, 128)
                first = homes[0, block, :]
                weight = [taps[k, block, :] for k in range(4)]
                for t in range(9):
                    if t < 8:
                        cell = rows16 + t * 16
                    else:
                        cell = jnp.where(rows16 < 2, rows16 + 128, jnp.where(rows16 == 2, -1, -1000))
                    value = picked(cell - first, weight)
                    high_part = value.astype(bf16)
                    whi[p, pl.ds(t * 16, 16), lanes] = high_part
                    wlo[p, pl.ds(t * 16, 16), lanes] = (value - high_part.astype(f32)).astype(bf16)
            whi[p, pl.ds(144, 112), :] = jnp.zeros((112, 256), bf16)
            wlo[p, pl.ds(144, 112), :] = jnp.zeros((112, 256), bf16)

    collide(pops)
    pl.semaphore_wait(barrier, len(all_dirs))
    first_copies = send_posts(0)
    prepare()
    build_weights(0, PAIRS // 2)
    stream(0, first_copies)
    collide(state.at[0])
    second_copies = send_posts(1)
    build_weights(PAIRS // 2, PAIRS)
    stream(1, second_copies)
    state_copy = pltpu.make_async_copy(state.at[1], state_hbm, out_sem)
    state_copy.start()

    for z in range(8):
        values = [state[1, i, tile_rows(z), :] for i in range(19)]
        flow = macroscopic(values)[1]
        for c in range(3):
            vmain[tile_rows(c * 8 + z), :] = flow[c]

    def sent_tile(region, k):
        dy, dz = region
        if region == (0, 0):
            return vmain[tile_rows(k), :]
        if dz == 0:
            start = (k // 2) * 64 + k % 2 if dy == -1 else k * 64 + 7
            return vmain[pl.ds(start, 8, stride=8), :]
        if dy == 0:
            tile = (k // 2) * 8 + k % 2 if dz == -1 else k * 8 + 7
            return vmain[tile_rows(tile), :]
        acc = jnp.zeros((8, 128), f32)
        for r, (c, y, z) in enumerate(corner_rows(region)[k * 8 : k * 8 + 8]):
            acc = jnp.where(sub == r, vmain[pl.ds(c * 64 + z * 8 + y, 1), :], acc)
        return acc

    v_copies = []
    number = 2 * N_POST
    for n, region in enumerate(region_list):
        first, count = region_span = regions[region]
        ahead = jnp.zeros((8, 128), f32)
        behind = jnp.zeros((8, 128), f32)
        for k in range(count):
            value = sent_tile(region, k)
            if region != (0, 0):
                vsend[tile_rows(first - 24 + k), :] = value
            behind = jnp.where((lane >> 1) == k, pltpu.roll(value, (2 * k) % 128, 1), behind)
            ahead = jnp.where(lane == k, pltpu.roll(value, (k - 127) % 128, 1), ahead)
        pksend[0, tile_rows(n), :] = behind
        pksend[1, tile_rows(n), :] = ahead
        if region != (0, 0):
            part = pl.ds((first - 24) * 8, count * 8)
            v_copies.append(
                copy(number, vsend.at[part], vmain.at[pl.ds(first * 8, count * 8)], (0,) + region)
            )
            number += 1
        for side, dx in ((0, -1), (1, 1)):
            part = pl.ds(n * 8, 8)
            v_copies.append(copy(number, pksend.at[side, part], pkrecv.at[side, part], (dx,) + region))
            number += 1

    facc[...] = jnp.zeros((ROWS, 256), f32)
    vmain[tile_rows(47), :] = jnp.zeros((8, 128), f32)
    vhalo[tile_rows(47), :] = jnp.zeros((8, 128), f32)
    for made in v_copies:
        made.wait_recv()
    for n, region in enumerate(region_list):
        first, count = regions[region]
        behind = pkrecv[0, tile_rows(n), :]
        ahead = pkrecv[1, tile_rows(n), :]
        for k in range(count):
            value = jnp.where(lane < 2, pltpu.roll(behind, (-2 * k) % 128, 1), 0.0)
            value = jnp.where(lane == 2, pltpu.roll(ahead, (2 - k) % 128, 1), value)
            vhalo[tile_rows(first + k), :] = value
    for t in range(ROWS // 16):
        rows = pl.ds(t * 16, 16)
        for source, lanes in ((vmain, pl.ds(0, 128)), (vhalo, pl.ds(128, 128))):
            value = source[rows, :]
            high_part = value.astype(bf16)
            vhi[rows, lanes] = high_part
            vlo[rows, lanes] = (value - high_part.astype(f32)).astype(bf16)

    @pl.loop(0, PAIRS)
    def _(p):
        w_high = whi[p]
        w_low = wlo[p]
        v_high = vhi[...]
        sampled_all = (
            jnp.dot(v_high, w_high, preferred_element_type=f32)
            + jnp.dot(v_high, w_low, preferred_element_type=f32)
            + jnp.dot(vlo[...], w_high, preferred_element_type=f32)
        )
        for j in range(2):
            lanes = pl.ds(j * 128, 128)
            b = 2 * p + j
            block = pl.ds(b, 1)
            t1 = sampled_all[:, j * 128 : (j + 1) * 128]

            def tile(t):
                return t1[t * 8 : t * 8 + 8, :]

            hy = homes[1, block, :]
            hz = homes[2, block, :]
            wy = [taps[4 + k, block, :] for k in range(4)]
            wz = [taps[8 + k, block, :] for k in range(4)]
            y_main = picked(sub - hy, wy)
            z_main = picked(sub - hz, wz)
            y_out = [picked(y - hy, wy) for y in (8, 9, -1)]
            z_out = [picked(z - hz, wz) for z in (8, 9, -1)]
            z_out = [jnp.where(at_top, 0.0, z_out[0]), jnp.where(at_top, 0.0, z_out[1]), jnp.where(at_bottom, 0.0, z_out[2])]
            even = (sub & 1) == 0
            y_pair = jnp.where(even, y_out[0], y_out[1])
            u_main = [y_main * z_main[z : z + 1, :] for z in range(8)]
            u_y = [z_main * y_out[k] for k in range(3)]
            u_z = [y_main * z_out[k] for k in range(3)]
            both = y_pair * jnp.where((sub & 2) == 0, z_out[0], z_out[1])
            u42 = both
            u43 = jnp.where(sub < 4, both, 0.0)
            u44 = jnp.where(sub < 6, y_out[2] * jnp.where(even, z_out[0], z_out[1]), 0.0)
            u45 = jnp.where(sub < 6, y_pair * z_out[2], 0.0)
            u46 = jnp.where(sub < 3, y_out[2] * z_out[2] + jnp.zeros((8, 128), f32), 0.0)
            p42 = tile(42) * u42
            p43 = tile(43) * u43
            p445 = tile(44) * u44 + tile(45) * u45
            p46 = tile(46) * u46
            alive = lax.broadcasted_iota(jnp.int32, (1, 128), 1) < counts[b]
            pushes = []
            rows = []
            for c in range(3):
                acc = jnp.where((sub >> 1) == c, p445, 0.0) + jnp.where(sub == c, p46, 0.0)
                if c < 2:
                    acc = acc + jnp.where((sub >> 2) == c, p42, 0.0)
                else:
                    acc = acc + p43
                for z in range(8):
                    acc = acc + tile(c * 8 + z) * u_main[z]
                acc = acc + tile(24 + c * 2) * u_y[0] + tile(25 + c * 2) * u_y[1] + tile(30 + c) * u_y[2]
                acc = acc + tile(33 + c * 2) * u_z[0] + tile(34 + c * 2) * u_z[1] + tile(39 + c) * u_z[2]
                sampled = jnp.sum(acc, axis=0, keepdims=True)
                speed = drop_vel[c, block, :]
                moved = speed + relax * (sampled - speed)
                pushes.append(jnp.where(alive, couple * (moved - sampled), 0.0))
                rows.append(jnp.where(alive, moved, 0.0))
            for c in range(3):
                rows.append(jnp.where(alive, drop_frac[c, block, :], 0.0) + rows[c])
            block_state = jnp.zeros((8, 128), f32)
            for c in range(6):
                block_state = jnp.where(sub == c, rows[c], block_state)
            states[pl.ds(pl.multiple_of(b * 8, 8), 8), :] = block_state

            by_half = jnp.where((sub >> 1) == 0, pushes[0], jnp.where((sub >> 1) == 1, pushes[1], pushes[2]))
            sources = [pushes[c] * u_main[z] for c in range(3) for z in range(8)]
            sources += [pushes[c] * u_y[k] for c in range(3) for k in range(2)]
            sources += [pushes[c] * u_y[2] for c in range(3)]
            sources += [pushes[c] * u_z[k] for c in range(3) for k in range(2)]
            sources += [pushes[c] * u_z[2] for c in range(3)]
            sources.append(jnp.where(sub < 4, pushes[0], pushes[1]) * u42)
            sources.append(pushes[2] * u43)
            sources.append(by_half * u44)
            sources.append(by_half * u45)
            sources.append(jnp.where(sub == 0, pushes[0], jnp.where(sub == 1, pushes[1], pushes[2])) * u46)
            sources.append(jnp.zeros((8, 128), f32))
            for t in range(ROWS // 16):
                value = jnp.concatenate([sources[2 * t], sources[2 * t + 1]], axis=0)
                high_part = value.astype(bf16)
                shi[pl.ds(t * 16, 16), lanes] = high_part
                slo[pl.ds(t * 16, 16), lanes] = (value - high_part.astype(f32)).astype(bf16)

        def over_droplets(source, weight):
            return lax.dot_general(source, weight, (((1,), (1,)), ((), ())), preferred_element_type=f32)

        s_high = shi[...]
        facc[...] += over_droplets(s_high, w_high) + over_droplets(s_high, w_low) + over_droplets(slo[...], w_high)

    codes = [dest[b] for b in range(BLOCKS)]
    wide = lax.broadcasted_iota(jnp.int32, (8, 128), 1)
    owner = wide >> 3
    code = jnp.zeros((8, 128), jnp.int32)
    for b in range(BLOCKS):
        code = jnp.where(owner == b, codes[b], code)
    rank = jnp.zeros((8, 128), jnp.int32)
    for b in range(BLOCKS):
        rank = rank + jnp.where((code == codes[b]) & (owner > b), 1, 0)
    lanes_of = jnp.where(code < 13, code, code - 1) * 2 + rank
    key = jnp.where(code == 13, -1, lanes_of * 8 + (wide & 7))[0:1, :]
    value = states[...]
    part_0 = value.astype(bf16)
    value = value - part_0.astype(f32)
    part_1 = value.astype(bf16)
    part_2 = (value - part_1.astype(f32)).astype(bf16)
    chosen = jnp.where(lax.broadcasted_iota(jnp.int32, (416, 128), 0) == key, 1.0, 0.0).astype(bf16)
    outbox[...] = (
        jnp.dot(chosen, part_0, preferred_element_type=f32)
        + jnp.dot(chosen, part_1, preferred_element_type=f32)
        + jnp.dot(chosen, part_2, preferred_element_type=f32)
    )
    h_copies = []
    for n, d in enumerate(all_dirs):
        part = pl.ds(n * 16, 16)
        h_copies.append(copy(number, outbox.at[part], inbox.at[part], d))
        number += 1

    f_copies = []
    for n, region in enumerate(region_list):
        first, count = regions[region]
        behind = jnp.zeros((8, 128), f32)
        ahead = jnp.zeros((8, 128), f32)
        for k in range(count):
            rows = tile_rows(first + k)
            if region != (0, 0):
                fsend[tile_rows(first - 24 + k), :] = facc[rows, 0:128]
            beyond = facc[rows, 128:256]
            behind = jnp.where((lane >> 1) == k, pltpu.roll(beyond, (2 * k) % 128, 1), behind)
            ahead = jnp.where(lane == k, pltpu.roll(beyond, (k - 2) % 128, 1), ahead)
        fpsend[0, tile_rows(n), :] = behind
        fpsend[1, tile_rows(n), :] = ahead
        back = (-region[0], -region[1])
        if region != (0, 0):
            part = pl.ds((first - 24) * 8, count * 8)
            f_copies.append(copy(number, fsend.at[part], frecv.at[part], (0,) + back))
            number += 1
        for side, dx in ((0, -1), (1, 1)):
            part = pl.ds(n * 8, 8)
            f_copies.append(copy(number, fpsend.at[side, part], fprecv.at[side, part], (-dx,) + back))
            number += 1

    stay_rows = lax.broadcasted_iota(jnp.int32, (16, 128), 0)
    stays = jnp.zeros((16, 128), jnp.int32)
    for b in range(BLOCKS):
        stays = jnp.where(stay_rows == b, codes[b], stays)
    for c in range(6):
        arrived[c, pl.ds(0, 16), :] = jnp.where(stays == 13, states[pl.ds(c, 16, stride=8), :], 0.0)

    for made in f_copies:
        made.wait_recv()
    for n, region in enumerate(region_list):
        first, count = regions[region]
        behind = fprecv[0, tile_rows(n), :]
        ahead = fprecv[1, tile_rows(n), :]
        for k in range(count):
            value = jnp.where(lane < 2, pltpu.roll(behind, (-2 * k) % 128, 1), 0.0)
            value = jnp.where(lane == 127, pltpu.roll(ahead, (127 - k) % 128, 1), value)
            rows = tile_rows(first + k)
            if region == (0, 0):
                facc[rows, 0:128] += value
            else:
                vhalo[rows, :] = frecv[tile_rows(first - 24 + k), :] + value

    def row_of(t, r):
        return vhalo[pl.ds(t * 8 + r, 1), :]

    def corner_row(region, c, y, z):
        return row_of(regions[region][0], corner_rows(region).index((c, y, z)))

    for c in range(3):
        for z in range(8):
            total = facc[tile_rows(c * 8 + z), 0:128]
            lines = [row_of(24 + c * 2, z), row_of(25 + c * 2, z), row_of(30 + c, z)]
            if z < 2 or z == 7:
                if z < 2:
                    total = total + vhalo[tile_rows(33 + c * 2 + z), :]
                    low, high = (-1, -1), (1, -1)
                else:
                    total = total + vhalo[tile_rows(39 + c), :]
                    low, high = (-1, 1), (1, 1)
                lines[0] = lines[0] + corner_row(low, c, 0, z)
                lines[1] = lines[1] + corner_row(low, c, 1, z)
                lines[2] = lines[2] + corner_row(high, c, 7, z)
            beside = jnp.where(sub == 0, lines[0], jnp.where(sub == 1, lines[1], jnp.where(sub == 7, lines[2], 0.0)))
            force[c, tile_rows(z), :] = total + beside

    for made in h_copies:
        made.wait_recv()
    for c in range(6):
        arrived[c, pl.ds(16, 52), :] = inbox[pl.ds(c, 52, stride=8), :]
    state_copy.wait()
    for made in started:
        made.wait_send()


def solution(mesh):
    sizes = tuple(mesh.shape[a] for a in ("gx", "gy", "gz"))

    def body(*refs):
        kernel(sizes, *refs)

    def local(pops, coarse_pops, interface, drop_vel, drop_frac, home, counts, dest):
        vmem = pl.BlockSpec(memory_space=pltpu.VMEM)
        smem = pl.BlockSpec(memory_space=pltpu.SMEM)
        state, force, arrived = pl.pallas_call(
            body,
            out_shape=(
                jax.ShapeDtypeStruct((19, 64, 128), f32),
                jax.ShapeDtypeStruct((3, 64, 128), f32),
                jax.ShapeDtypeStruct((6, 68, 128), f32),
            ),
            in_specs=[vmem] * 6 + [smem] * 2,
            out_specs=(pl.BlockSpec(memory_space=pl.ANY), vmem, vmem),
            scratch_shapes=[
                pltpu.VMEM((19, 64, 128), f32),
                pltpu.VMEM((2, 19, 64, 128), f32),
                pltpu.VMEM((2, POST_TILES * 8, 128), f32),
                pltpu.VMEM((2, POST_TILES * 8, 128), f32),
                pltpu.VMEM((ROWS, 128), f32),
                pltpu.VMEM((ROWS, 128), f32),
                pltpu.VMEM((24 * 8, 128), f32),
                pltpu.VMEM((2, 72, 128), f32),
                pltpu.VMEM((2, 72, 128), f32),
                pltpu.VMEM((ROWS, 256), bf16),
                pltpu.VMEM((ROWS, 256), bf16),
                pltpu.VMEM((PAIRS, 256, 256), bf16),
                pltpu.VMEM((PAIRS, 256, 256), bf16),
                pltpu.VMEM((12, 16, 128), f32),
                pltpu.VMEM((3, 16, 128), jnp.int32),
                pltpu.VMEM((ROWS, 256), bf16),
                pltpu.VMEM((ROWS, 256), bf16),
                pltpu.VMEM((ROWS, 256), f32),
                pltpu.VMEM((24 * 8, 128), f32),
                pltpu.VMEM((24 * 8, 128), f32),
                pltpu.VMEM((2, 72, 128), f32),
                pltpu.VMEM((2, 72, 128), f32),
                pltpu.VMEM((BLOCKS * 8, 128), f32),
                pltpu.VMEM((416, 128), f32),
                pltpu.VMEM((416, 128), f32),
                pltpu.SemaphoreType.DMA((N_MSG,)),
                pltpu.SemaphoreType.DMA((N_MSG,)),
                pltpu.SemaphoreType.DMA,
            ],
            compiler_params=pltpu.CompilerParams(collective_id=0, has_side_effects=True),
            name="channel",
        )(
            pops.reshape(19, 64, 128),
            coarse_pops,
            interface,
            drop_vel,
            drop_frac,
            home,
            counts,
            dest,
        )
        return state.reshape(19, 8, 8, 128), force.reshape(3, 8, 8, 128), arrived

    return jax.shard_map(
        local,
        mesh=mesh,
        in_specs=(
            P(None, "gz", "gy", "gx"),
            P(None, "gz", "gy", "gx"),
            P("gz", "gy", "gx"),
            P(None, ("gx", "gy", "gz"), None),
            P(None, ("gx", "gy", "gz"), None),
            P(("gx", "gy", "gz"), None),
            P(("gx", "gy", "gz")),
            P(("gx", "gy", "gz")),
        ),
        out_specs=(
            P(None, "gz", "gy", "gx"),
            P(None, "gz", "gy", "gx"),
            P(None, ("gx", "gy", "gz"), None),
        ),
        check_vma=False,
    )
```

time: 330 us -> 60.4 us (0.18); the launches traced: 325 us -> 60.2 us
  local copies, waits for them, and re-layouts: 103 us -> 3.34 us
  starting transfers between devices: 93.9 us -> 0 us
  Pallas kernels: 0 us -> 56.2 us
  loops' own time: 44.4 us -> 0 us
  waiting for transfers between devices: 38.6 us -> 0 us
  other arithmetic: 27.8 us -> 0 us
  matrix products: 16.3 us -> 0 us
    ppermute x30 -> x0, starting transfers between devices: 93.9 us -> none  [the longest x15 55.7 us: with_halo(): lax.ppermute(head, axis, [((i + 1) % count, i) for i in range(count)])]
    dynamic_update_slice x20 -> x0, local copies, waits for them, and re-layouts: 88.8 us -> none  [the longest x16 88.7 us: droplet_group(): lax.dynamic_update_slice(spread, lax.dynamic_slice(spread, corner, (3, ed...]
    pallas_call x0 -> x1, Pallas kernels: none -> 56.2 us  [local(): pl.pallas_call(body, out_shape=(jax.ShapeDtypeStruct((19, 64, 128), f32),...]
    another operation x1 -> x0, loops' own time: 44.4 us -> none  [local(): lax.scan(droplet_group, jnp.zeros_like(velocity_ext), (homes, speeds, fra...]
    ppermute x30 -> x0, waiting for transfers between devices: 38.6 us -> none  [the longest x15 21.1 us: with_halo(): lax.ppermute(head, axis, [((i + 1) % count, i) for i in range(count)])]
    dot_general x32 -> x0, matrix products: 16.3 us -> none  [the longest x16 8.3 us: droplet_group(): jnp.dot(tile.reshape(3 * edge * edge, edge), weight_x.T, precision=highest)]
    unnamed x36 -> x0, other arithmetic: 15.7 us -> none
    slice x17 -> x0, local copies, waits for them, and re-layouts: 5.38 us -> none  [the longest x4 2.41 us: droplet_group(): first = cells[0]]
  transfers between devices with their start and end apart: 30 -> 0, of which waited for: 21 -> 0; matrix products, arithmetic and copies ran while one was open for 2% -> 0% of each run, Pallas kernels for 0% -> 0%
where the time goes in v1:
time: 60.4 us; the launch traced here: 60.2 us
  Pallas kernels  56.2 us (93%)
  local copies, waits for them, and re-layouts  3.34 us (6%)
  between operations  0.66 us (1%)
    pallas_call x1, Pallas kernels, local(): pl.pallas_call(body, out_shape=(jax.ShapeDtypeStruct((19, 64, 128), f32),...  56.2 us
    unnamed x7, local copies, waits for them, and re-layouts  3.34 us

profile of v1, /device:TPU:1, one launch (start us, length us, event | category | flops | bytes accessed | tf_op | source)
XLA Modules:
  0.0 60.2 jit_solution(7775373537293933192)
XLA Ops:
  0.6 56.2 %channel.1 = (f32[19,64,128]{2,1,0:T(8,128)}, f32[3,64,128]{2,1,0:T(8,128)}, f32[6,68,128]{2,1,0:T(8,128)}) custom-call(f32[19,64,128]{2,1,0:T(8,128)} %bitcast.3, bf16[19,8,8,128]{3,2,1,0:T(8,128)(2,1)} %refs_1_.1, s32[8,8,128]{2,1,0:T(8,128)} %refs_2_.1, f32[3,16,128]{2,1,0:T(8,128)} %refs_3_.1, f32[3,16,128]{2,1,0:T(8,128)} %refs_4_.1, ...), custom_call_target="tpu_custom_call" | custom-call | tf_op jit(solution)/shard_map/channel/pallas_call | solution.py:572
  56.8 0.0 copy-start.1
  56.9 0.0 copy-start
  56.9 2.0 %copy.14 = f32[19,8,8,128]{3,2,1,0:T(8,128)} copy(f32[19,8,8,128]{3,2,1,0:T(8,128)} %bitcast.4) | data formatting | bytes 1245184
  58.9 0.0 copy-done.1
  58.9 0.6 %copy.15 = f32[3,8,8,128]{3,2,1,0:T(8,128)} copy(f32[3,8,8,128]{3,2,1,0:T(8,128)S(1)} %bitcast.5) | data formatting | bytes 196608
  59.5 0.0 copy-done
  59.5 0.7 %copy.16 = f32[6,68,128]{2,1,0:T(8,128)} copy(f32[6,68,128]{2,1,0:T(8,128)S(1)} %copy-done) | data formatting | bytes 417792
Async XLA Ops:
  56.8 2.0 %copy-start.1 = (f32[3,64,128]{2,1,0:T(8,128)S(1)}, f32[3,64,128]{2,1,0:T(8,128)}, u32[]{:S(2)}) copy-start(f32[3,64,128]{2,1,0:T(8,128)} %get-tuple-element.7) | copy-start | bytes 294916
  56.9 2.7 %copy-start = (f32[6,68,128]{2,1,0:T(8,128)S(1)}, f32[6,68,128]{2,1,0:T(8,128)}, u32[]{:S(2)}) copy-start(f32[6,68,128]{2,1,0:T(8,128)} %get-tuple-element.14) | copy-start | bytes 626692

commit v2 on v1

v2 whole, which is shorter than its diff:
```python
import math

import jax
import jax.numpy as jnp
import numpy as np
from jax import lax
from jax.experimental import pallas as pl
from jax.experimental.pallas import tpu as pltpu
from jax.sharding import PartitionSpec as P

lattice = [
    (0, 0, 0), (1, 0, 0), (-1, 0, 0), (0, 1, 0), (0, -1, 0), (0, 0, 1), (0, 0, -1),
    (1, 1, 0), (-1, -1, 0), (1, -1, 0), (-1, 1, 0), (1, 0, 1), (-1, 0, -1), (1, 0, -1),
    (-1, 0, 1), (0, 1, 1), (0, -1, -1), (0, 1, -1), (0, -1, 1),
]
weights_table = [1.0 / 3.0] + [1.0 / 18.0] * 6 + [1.0 / 36.0] * 12
opposite = [0, 2, 1, 4, 3, 6, 5, 8, 7, 10, 9, 12, 11, 14, 13, 16, 15, 18, 17]
inverse_tau = 0.8
relax = 0.5
couple = 8.0
f32 = jnp.float32
bf16 = jnp.bfloat16

face_pops = {}
for axis in range(3):
    for sign in (1, -1):
        d = [0, 0, 0]
        d[axis] = sign
        face_pops[tuple(d)] = [i for i in range(19) if lattice[i][axis] == sign]
post_msgs = {}
tiles = 0
for i in list(range(7, 19)) + [3, 4, 5, 6, 1, 2]:
    c = lattice[i]
    count = 1 if (abs(c[0]) + abs(c[1]) + abs(c[2]) > 1 or c[0] != 0) else 5
    post_msgs[c] = (tiles, count)
    tiles += count
POST_TILES = tiles

regions = {
    (0, 0): (0, 24),
    (-1, 0): (24, 6),
    (1, 0): (30, 3),
    (0, -1): (33, 6),
    (0, 1): (39, 3),
    (-1, -1): (42, 2),
    (1, -1): (44, 1),
    (-1, 1): (45, 1),
    (1, 1): (46, 1),
}
region_list = list(regions)[::-1]
ROWS = 48 * 8
all_dirs = [(x, y, z) for z in (-1, 0, 1) for y in (-1, 0, 1) for x in (-1, 0, 1) if (x, y, z) != (0, 0, 0)]
far_first = sorted(all_dirs, key=lambda d: -abs(d[0]) - abs(d[1]) - abs(d[2]))
U_TILES = 19
WIDE = 2048
N_POST = 18
N_MSG = 2 * N_POST + 3 * 26
PAIRS = 8
BLOCKS = 16
UNROLL = 4
GROUP = 12


def corner_rows(region):
    dy, dz = region
    ys = [7] if dy == 1 else [0, 1]
    zs = [7] if dz == 1 else [0, 1]
    return [(c, y, z) for c in range(3) for z in zs for y in ys]


def tile_rows(t):
    return pl.ds(t * 8, 8)


def kernel(
    sizes,
    pops_hbm, coarse_hbm, interface_hbm, drop_vel_hbm, drop_frac_hbm, home_hbm, counts_hbm, dest_hbm,
    state_out, force, arrived,
    pops, coarse, interface, drop_vel, drop_frac, home, counts, dest,
    posts, state_mid, psend, precv, vmain, vsend, pksend, pkrecv, va, vb, weights,
    taps, homes, spread_weights, tmain, shi, slo, f_main, f_beyond, fsend, frecv, fpsend, fprecv, states, outbox, inbox,
    send_sem, recv_sem, in_sem,
):
    n_x, n_y, n_z = sizes
    me = (lax.axis_index("gx"), lax.axis_index("gy"), lax.axis_index("gz"))
    level = me[2]
    at_bottom = level == 0
    at_top = level == n_z - 1

    def moved_by(axis, step, size):
        if step == 0:
            return me[axis]
        return lax.rem(me[axis] + (step + size), size)

    coords = {
        (axis, step): moved_by(axis, step, size)
        for axis, size in enumerate(sizes)
        for step in (-1, 0, 1)
    }

    def device(d):
        return {"gx": coords[0, d[0]], "gy": coords[1, d[1]], "gz": coords[2, d[2]]}

    lane = lax.broadcasted_iota(jnp.int32, (8, 128), 1)
    sub = lax.broadcasted_iota(jnp.int32, (8, 128), 0)

    third = (lane * 171) >> 9
    outer_low = lane - third * 3 == 0
    started = []

    def copy(index, src, dst, d):
        made = pltpu.make_async_remote_copy(
            src_ref=src,
            dst_ref=dst,
            send_sem=send_sem.at[index],
            recv_sem=recv_sem.at[index],
            device_id=device(d),
            device_id_type=pl.DeviceIdType.MESH,
        )
        made.start()
        started.append(made)
        return made

    loads = []
    for n, (src, dst) in enumerate(
        (
            (pops_hbm, pops),
            (coarse_hbm, coarse),
            (interface_hbm, interface),
            (drop_vel_hbm, drop_vel),
            (drop_frac_hbm, drop_frac),
            (home_hbm, home),
            (counts_hbm, counts),
            (dest_hbm, dest),
        )
    ):
        loads.append(pltpu.make_async_copy(src, dst, in_sem.at[n]))
        loads[-1].start()
    barrier = pltpu.get_barrier_semaphore()
    for d in far_first:
        pl.semaphore_signal(barrier, inc=1, device_id=device(d), device_id_type=pl.DeviceIdType.MESH)

    def macroscopic(values):
        plus = {i: values[i] + values[i + 1] for i in range(1, 19, 2)}
        minus = {i: values[i] - values[i + 1] for i in range(1, 19, 2)}
        axes = plus[1] + plus[3] + plus[5]
        edges = (plus[7] + plus[9]) + (plus[11] + plus[13]) + (plus[15] + plus[17])
        density = values[0] * weights_table[0] + axes * weights_table[1] + edges * weights_table[7]
        inverse = 1.0 / density
        near, far = weights_table[1] * inverse, weights_table[7] * inverse
        flow = [
            minus[1] * near + ((minus[7] + minus[9]) + (minus[11] + minus[13])) * far,
            minus[3] * near + ((minus[7] - minus[9]) + (minus[15] + minus[17])) * far,
            minus[5] * near + ((minus[11] - minus[13]) + (minus[15] - minus[17])) * far,
        ]
        return density, flow

    def collide(source):
        @pl.loop(0, 8)
        def _(z):
            rows = pl.ds(pl.multiple_of(z * 8, 8), 8)
            values = [source[i, rows, :] for i in range(19)]
            density, flow = macroscopic(values)
            square = flow[0] * flow[0] + flow[1] * flow[1] + flow[2] * flow[2]
            inside = interface[z] == 1
            scaled = density * inverse_tau
            base = scaled - square * (1.5 * scaled)
            first, second = scaled * 3.0, scaled * 4.5

            def put(i, balance):
                relaxed = values[i] * (1.0 - inverse_tau) + balance
                posts[i, rows, :] = jnp.where(inside, coarse[i, z].astype(f32), relaxed)

            put(0, base)
            for i in range(1, 19, 2):
                along = None
                for axis in range(3):
                    sign = lattice[i][axis]
                    if sign == 1:
                        along = flow[axis] if along is None else along + flow[axis]
                    if sign == -1:
                        along = along - flow[axis]
                even = base + along * along * second
                odd = along * first
                put(i, even + odd)
                put(i + 1, even - odd)

    def send_posts(r):
        copies = {}
        for number, (d, (first, count)) in enumerate(post_msgs.items()):
            layer = {a: (7 if d[a] == 1 else 0) for a in (1, 2)}
            if d in face_pops:
                listed = face_pops[d]
            else:
                listed = [lattice.index(d)]
            if d[0] != 0 and d[1] == 0 and d[2] == 0:
                acc = jnp.zeros((8, 128), f32)
                from_lane = 127 if d[0] == 1 else 0
                for k, i in enumerate(listed):
                    for z in range(8):
                        spot = k * 8 + z
                        turned = pltpu.roll(posts[i, tile_rows(z), :], (spot - from_lane) % 128, 1)
                        acc = jnp.where(lane == spot, turned, acc)
                psend[r, tile_rows(first), :] = acc
            elif d[2] != 0:
                for k, i in enumerate(listed):
                    psend[r, tile_rows(first + k), :] = posts[i, tile_rows(layer[2]), :]
            else:
                for k, i in enumerate(listed):
                    psend[r, tile_rows(first + k), :] = posts[i, pl.ds(layer[1], 8, stride=8), :]
            part = pl.ds(first * 8, count * 8)
            copies[d] = copy(r * N_POST + number, psend.at[r, part], precv.at[r, part], d)
        return copies

    def pull(r, i):
        cx, cy, cz = lattice[i]
        far = 127 if cx == 1 else 0

        def halo(d):
            first, count = post_msgs[d]
            k = face_pops[d].index(i) if d in face_pops and d[0] == 0 else 0
            return first + k

        def x_shift(value, beyond):
            return pltpu.roll(jnp.where(lane == far, beyond, value), cx % 128, 1)

        def y_shift(value, row):
            edge = 0 if cy == 1 else 7
            return jnp.where(sub == edge, row, pltpu.roll(value, cy % 8, 0))

        wanted = [z - cz for z in range(8)]
        planes = {z: posts[i, tile_rows(z), :] for z in range(8) if z in wanted}
        outer = None
        if cz != 0:
            outer = precv[r, tile_rows(halo((0, 0, cz))), :]
        if cx != 0:
            packed = precv[r, tile_rows(post_msgs[(cx, 0, 0)][0]), :]
            k = face_pops[(cx, 0, 0)].index(i)
            for z in planes:
                planes[z] = x_shift(planes[z], pltpu.roll(packed, (far - (k * 8 + z)) % 128, 1))
            if cz != 0:
                outer = x_shift(outer, precv[r, tile_rows(halo((cx, 0, cz))), :])
        if cy != 0:
            place = halo((0, cy, 0))
            if cx != 0:
                side = x_shift(precv[r, tile_rows(place), :], precv[r, tile_rows(halo((cx, cy, 0))), :])
                for z in planes:
                    planes[z] = y_shift(planes[z], side[z : z + 1, :])
            else:
                for z in planes:
                    planes[z] = y_shift(planes[z], precv[r, pl.ds(place * 8 + z, 1), :])
            if cz != 0:
                row = halo((0, cy, cz)) * 8 + (7 if cy == 1 else 0)
                outer = y_shift(outer, precv[r, pl.ds(row, 1), :])
        out = [planes[z] if z in planes else outer for z in wanted]
        if cz == 1:
            out[0] = jnp.where(at_bottom, posts[opposite[i], tile_rows(0), :], out[0])
        if cz == -1:
            out[7] = jnp.where(at_top, posts[opposite[i], tile_rows(7), :], out[7])
        return out

    def stream(r, copies, into):
        for made in copies.values():
            made.wait_recv()
        for i in range(19):
            out = pull(r, i)
            for z in range(8):
                into[i, tile_rows(z), :] = out[z]

    def prepare():
        for axis in range(3):
            angle = drop_frac[axis] * (0.5 * math.pi)
            sine = jnp.sin(angle)
            cosine = jnp.cos(angle)
            taps[axis * 4 + 0] = 0.25 - 0.25 * sine
            taps[axis * 4 + 1] = 0.25 + 0.25 * cosine
            taps[axis * 4 + 2] = 0.25 + 0.25 * sine
            taps[axis * 4 + 3] = 0.25 - 0.25 * cosine
        cells = home[...]
        homes[0] = (cells & 127) - 1
        homes[1] = ((cells >> 7) & 7) - 1
        homes[2] = (cells >> 10) - 1

    def picked(offset, weight):
        zero = jnp.zeros(offset.shape, f32)
        return jnp.where(
            offset == 0,
            weight[0],
            jnp.where(offset == 1, weight[1], jnp.where(offset == 2, weight[2], jnp.where(offset == 3, weight[3], zero))),
        )

    rows16 = lax.broadcasted_iota(jnp.int32, (16, 128), 0)

    def build_x_weights():
        @pl.loop(0, BLOCKS)
        def _(b):
            block = pl.ds(b, 1)
            lanes = pl.ds(pl.multiple_of(b * 128, 128), 128)
            first = homes[0, block, :]
            weight = [taps[k, block, :] for k in range(4)]
            for t in range(8):
                value = picked(rows16 + t * 16 - first, weight)
                high_part = value.astype(bf16)
                weights[pl.ds(t * 16, 16), lanes] = high_part
                weights[pl.ds(128 + t * 16, 16), lanes] = (value - high_part.astype(f32)).astype(bf16)
            def outside(at):
                row = rows16 - at
                cell = jnp.where(row == 0, -1, jnp.where(row == 1, 128, jnp.where(row == 2, 129, -1000)))
                return picked(cell - first, weight)

            value = outside(0)
            high_part = value.astype(bf16)
            weights[pl.ds(256, 16), lanes] = high_part
            weights[pl.ds(272, 16), lanes] = jnp.zeros((16, 128), bf16)
            weights[pl.ds(288, 16), lanes] = outside(8).astype(bf16)
            weights[pl.ds(304, 32), lanes] = jnp.zeros((32, 128), bf16)
            weights[pl.ds(336, 16), lanes] = (value - high_part.astype(f32)).astype(bf16)
            weights[pl.ds(352, 32), lanes] = jnp.zeros((32, 128), bf16)

    def build_yz_weights():
        @pl.loop(0, BLOCKS)
        def _(b):
            block = pl.ds(b, 1)
            hy = homes[1, block, :]
            hz = homes[2, block, :]
            wy = [taps[4 + k, block, :] for k in range(4)]
            wz = [taps[8 + k, block, :] for k in range(4)]
            y_main = picked(sub - hy, wy)
            z_main = picked(sub - hz, wz)
            y_out = [picked(y - hy, wy) for y in (8, 9, -1)]
            z_out = [picked(z - hz, wz) for z in (8, 9, -1)]
            z_out = [jnp.where(at_top, 0.0, z_out[0]), jnp.where(at_top, 0.0, z_out[1]), jnp.where(at_bottom, 0.0, z_out[2])]
            even = (sub & 1) == 0
            y_pair = jnp.where(even, y_out[0], y_out[1])
            z_pair = jnp.where(even, z_out[0], z_out[1])
            both = y_pair * jnp.where((sub & 2) == 0, z_out[0], z_out[1])
            made = [y_main * z_main[z : z + 1, :] for z in range(8)]
            made += [z_main * y_out[k] for k in range(3)]
            made += [y_main * z_out[k] for k in range(3)]
            made.append(both)
            made.append(jnp.where(sub < 4, both, 0.0))
            made.append(jnp.where(sub < 6, y_out[2] * z_pair, 0.0))
            made.append(jnp.where(sub < 6, y_pair * z_out[2], 0.0))
            made.append(jnp.where(sub < 3, y_out[2] * z_out[2], 0.0))
            for t in range(U_TILES):
                spread_weights[b, tile_rows(t), :] = made[t]

    for made in loads[:3]:
        made.wait()
    collide(pops)
    pl.semaphore_wait(barrier, len(all_dirs))
    first_copies = send_posts(0)
    stream(0, first_copies, state_mid)
    collide(state_mid)
    second_copies = send_posts(1)
    for made in loads[3:]:
        made.wait()
    prepare()
    build_x_weights()
    build_yz_weights()
    stream(1, second_copies, state_out)

    for z in range(8):
        values = [state_out[i, tile_rows(z), :] for i in range(19)]
        flow = macroscopic(values)[1]
        for c in range(3):
            vmain[tile_rows(c * 8 + z), :] = flow[c]

    def sent_tile(region, k):
        dy, dz = region
        if region == (0, 0):
            return vmain[tile_rows(k), :]
        if dz == 0:
            start = (k // 2) * 64 + k % 2 if dy == -1 else k * 64 + 7
            return vmain[pl.ds(start, 8, stride=8), :]
        if dy == 0:
            tile = (k // 2) * 8 + k % 2 if dz == -1 else k * 8 + 7
            return vmain[tile_rows(tile), :]
        acc = jnp.zeros((8, 128), f32)
        for r, (c, y, z) in enumerate(corner_rows(region)[k * 8 : k * 8 + 8]):
            acc = jnp.where(sub == r, vmain[pl.ds(c * 64 + z * 8 + y, 1), :], acc)
        return acc

    v_copies = []
    number = 2 * N_POST
    for n, region in enumerate(region_list):
        first, count = regions[region]
        packed = jnp.zeros((8, 128), f32)
        for k in range(count):
            value = sent_tile(region, k)
            if region != (0, 0):
                vsend[tile_rows(first - 24 + k), :] = value
            packed = jnp.where(third == k, pltpu.roll(value, 3 * k + 1, 1), packed)
        pksend[tile_rows(n), :] = packed
        for side, dx in ((0, -1), (1, 1)):
            part = pl.ds(n * 8, 8)
            v_copies.append(copy(number, pksend.at[part], pkrecv.at[side, part], (dx,) + region))
            number += 1
        if region != (0, 0):
            part = pl.ds((first - 24) * 8, count * 8)
            v_copies.append(
                copy(number, vsend.at[part], vmain.at[pl.ds(first * 8, count * 8)], (0,) + region)
            )
            number += 1

    def split_main(low, high):
        for t in range(low, high):
            rows = pl.ds(t * 16, 16)
            value = vmain[rows, :]
            high_part = value.astype(bf16)
            va[rows, pl.ds(0, 128)] = high_part
            vb[rows, pl.ds(0, 128)] = high_part
            va[rows, pl.ds(128, 128)] = (value - high_part.astype(f32)).astype(bf16)

    vmain[tile_rows(47), :] = jnp.zeros((8, 128), f32)
    split_main(0, 12)

    @pl.loop(0, PAIRS)
    def _(p):
        lanes = pl.ds(pl.multiple_of(p * 256, 256), 256)
        w_high = weights[pl.ds(0, 128), lanes]
        tmain[p] = jnp.dot(va[pl.ds(0, 192), :], jnp.concatenate([w_high, w_high], axis=0), preferred_element_type=f32)

    waited = len(started) - len(v_copies)
    for made in started[:waited]:
        made.wait_send()
    for made in v_copies:
        made.wait_recv()
    split_main(12, 24)
    beyond = {}
    for n, region in enumerate(region_list):
        first, count = regions[region]
        merged = jnp.where(outer_low, pkrecv[1, tile_rows(n), :], pkrecv[0, tile_rows(n), :])
        for g in range(0, count, GROUP):
            value = merged if g == 0 else pltpu.roll(merged, (-3 * g) % 128, 1)
            high_part = value.astype(bf16).astype(f32)
            low_part = pltpu.roll(value - high_part, 40, 1)
            value = jnp.where(lane < 40, high_part, jnp.where(lane < 80, low_part, pltpu.roll(high_part, 80, 1)))
            for k in range(g, min(g + GROUP, count)):
                beyond[first + k] = pltpu.roll(value, (-3 * (k - g)) % 128, 1) if k > g else value
    beyond[47] = jnp.zeros((8, 128), f32)
    for t in range(ROWS // 16):
        vb[pl.ds(t * 16, 16), pl.ds(128, 128)] = jnp.concatenate([beyond[2 * t], beyond[2 * t + 1]], axis=0).astype(bf16)

    @pl.loop(0, PAIRS, unroll=UNROLL)
    def _(p):
        pair_lanes = pl.ds(pl.multiple_of(p * 256, 256), 256)
        w_high = weights[pl.ds(0, 128), pair_lanes]
        w_rest = weights[pl.ds(128, 256), pair_lanes]
        t_main = tmain[p] + jnp.dot(vb[pl.ds(0, 192), :], w_rest, preferred_element_type=f32)
        t_out = jnp.dot(
            va[pl.ds(192, 192), :], jnp.concatenate([w_high, w_high], axis=0), preferred_element_type=f32
        ) + jnp.dot(vb[pl.ds(192, 192), :], w_rest, preferred_element_type=f32)
        for j in range(2):
            b = 2 * p + j
            lanes = pl.ds(pl.multiple_of(p * 256 + j * 128, 128), 128)
            block = pl.ds(b, 1)

            def tile(t):
                source, at = (t_main, t) if t < 24 else (t_out, t - 24)
                return source[at * 8 : at * 8 + 8, j * 128 : (j + 1) * 128]

            def u(t):
                return spread_weights[b, tile_rows(t), :]

            p42 = tile(42) * u(14)
            p43 = tile(43) * u(15)
            p445 = tile(44) * u(16) + tile(45) * u(17)
            p46 = tile(46) * u(18)
            alive = lax.broadcasted_iota(jnp.int32, (1, 128), 1) < counts[b]
            pushes = []
            rows = []
            for c in range(3):
                acc = jnp.where((sub >> 1) == c, p445, 0.0) + jnp.where(sub == c, p46, 0.0)
                if c < 2:
                    acc = acc + jnp.where((sub >> 2) == c, p42, 0.0)
                else:
                    acc = acc + p43
                other = tile(c * 8) * u(0)
                for z in range(1, 8):
                    other = other + tile(c * 8 + z) * u(z)
                acc = acc + tile(24 + c * 2) * u(8) + tile(25 + c * 2) * u(9) + tile(30 + c) * u(10)
                acc = acc + tile(33 + c * 2) * u(11) + tile(34 + c * 2) * u(12) + tile(39 + c) * u(13)
                sampled = jnp.sum(acc + other, axis=0, keepdims=True)
                speed = drop_vel[c, block, :]
                moved = speed + relax * (sampled - speed)
                pushes.append(jnp.where(alive, couple * (moved - sampled), 0.0))
                rows.append(jnp.where(alive, moved, 0.0))
            for c in range(3):
                rows.append(jnp.where(alive, drop_frac[c, block, :], 0.0) + rows[c])
            block_state = jnp.zeros((8, 128), f32)
            for c in range(6):
                block_state = jnp.where(sub == c, rows[c], block_state)
            states[pl.ds(pl.multiple_of(b * 8, 8), 8), :] = block_state

            by_half = jnp.where((sub >> 1) == 0, pushes[0], jnp.where((sub >> 1) == 1, pushes[1], pushes[2]))
            by_row = jnp.where(sub == 0, pushes[0], jnp.where(sub == 1, pushes[1], pushes[2]))
            by_four = jnp.where(sub < 4, pushes[0], pushes[1])
            plan = [(pushes[c], z) for c in range(3) for z in range(8)]
            plan += [(pushes[c], 8 + k) for c in range(3) for k in range(2)]
            plan += [(pushes[c], 10) for c in range(3)]
            plan += [(pushes[c], 11 + k) for c in range(3) for k in range(2)]
            plan += [(pushes[c], 13) for c in range(3)]
            plan += [(by_four, 14), (pushes[2], 15), (by_half, 16), (by_half, 17), (by_row, 18)]
            sources = [push * u(t) for push, t in plan] + [jnp.zeros((8, 128), f32)]
            for t in range(ROWS // 16):
                value = jnp.concatenate([sources[2 * t], sources[2 * t + 1]], axis=0)
                high_part = value.astype(bf16)
                shi[pl.ds(t * 16, 16), lanes] = high_part
                slo[pl.ds(t * 16, 16), lanes] = (value - high_part.astype(f32)).astype(bf16)

    codes = [dest[b] for b in range(BLOCKS)]
    wide = lax.broadcasted_iota(jnp.int32, (8, 128), 1)
    owner = wide >> 3
    code = jnp.zeros((8, 128), jnp.int32)
    for b in range(BLOCKS):
        code = jnp.where(owner == b, codes[b], code)
    rank = jnp.zeros((8, 128), jnp.int32)
    for b in range(BLOCKS):
        rank = rank + jnp.where((code == codes[b]) & (owner > b), 1, 0)
    lanes_of = jnp.where(code < 13, code, code - 1) * 2 + rank
    key = jnp.where(code == 13, -1, lanes_of * 8 + (wide & 7))[0:1, :]
    value = states[...]
    part_0 = value.astype(bf16)
    value = value - part_0.astype(f32)
    part_1 = value.astype(bf16)
    part_2 = (value - part_1.astype(f32)).astype(bf16)
    chosen = jnp.where(lax.broadcasted_iota(jnp.int32, (416, 128), 0) == key, 1.0, 0.0).astype(bf16)
    outbox[...] = (
        jnp.dot(chosen, part_0, preferred_element_type=f32)
        + jnp.dot(chosen, part_1, preferred_element_type=f32)
        + jnp.dot(chosen, part_2, preferred_element_type=f32)
    )
    def over_droplets(source, weight):
        return lax.dot_general(source, weight, (((1,), (1,)), ((), ())), preferred_element_type=f32)

    near = over_droplets(shi[...], weights[pl.ds(0, 256), :])
    last = over_droplets(slo[...], jnp.concatenate([weights[pl.ds(0, 128), :], weights[pl.ds(256, 128), :]], axis=0))
    f_main[...] = near[:, 0:128] + near[:, 128:256] + last[:, 0:128]
    part_high = over_droplets(shi[...], weights[pl.ds(256, 128), :])
    f_beyond[...] = part_high + last[:, 128:256]
    shifted = lane - 80
    spot = jnp.where(lane < 36, third, jnp.where((lane >= 80) & (lane < 116), (shifted * 171) >> 9, -1))

    f_copies = []
    for n, region in enumerate(region_list):
        first, count = regions[region]
        packed = None
        for g in range(0, count, GROUP):
            value = jnp.zeros((8, 128), f32)
            for k in range(g, min(g + GROUP, count)):
                rows = tile_rows(first + k)
                if region != (0, 0):
                    fsend[tile_rows(first - 24 + k), :] = f_main[rows, :]
                both = f_beyond[rows, :]
                value = jnp.where(spot == k - g, pltpu.roll(both, 3 * (k - g), 1) if k > g else both, value)
            value = value + pltpu.roll(value, 48, 1)
            packed = value if g == 0 else jnp.where(lane < 3 * g, packed, pltpu.roll(value, 3 * g, 1))
        fpsend[tile_rows(n), :] = packed
        back = (-region[0], -region[1])
        for side, dx in ((0, -1), (1, 1)):
            part = pl.ds(n * 8, 8)
            f_copies.append(copy(number, fpsend.at[part], fprecv.at[side, part], (-dx,) + back))
            number += 1
        if region != (0, 0):
            part = pl.ds((first - 24) * 8, count * 8)
            f_copies.append(copy(number, fsend.at[part], frecv.at[part], (0,) + back))
            number += 1

    h_copies = []
    for d in far_first:
        part = pl.ds(all_dirs.index(d) * 16, 16)
        h_copies.append(copy(number, outbox.at[part], inbox.at[part], d))
        number += 1

    stay_rows = lax.broadcasted_iota(jnp.int32, (16, 128), 0)
    stays = jnp.zeros((16, 128), jnp.int32)
    for b in range(BLOCKS):
        stays = jnp.where(stay_rows == b, codes[b], stays)
    for c in range(6):
        arrived[c, pl.ds(0, 16), :] = jnp.where(stays == 13, states[pl.ds(c, 16, stride=8), :], 0.0)

    for made in started[waited : waited + len(v_copies)]:
        made.wait_send()
    for made in f_copies:
        made.wait_recv()
    for n, region in enumerate(region_list):
        first, count = regions[region]
        merged = jnp.where(outer_low, fprecv[1, tile_rows(n), :], fprecv[0, tile_rows(n), :])
        for k in range(count):
            value = jnp.where((lane < 2) | (lane == 127), pltpu.roll(merged, (127 - 3 * k) % 128, 1), 0.0)
            rows = tile_rows(first + k)
            if region == (0, 0):
                f_main[rows, :] += value
            else:
                vmain[rows, :] = frecv[tile_rows(first - 24 + k), :] + value

    def row_of(t, r):
        return vmain[pl.ds(t * 8 + r, 1), :]

    def corner_row(region, c, y, z):
        return row_of(regions[region][0], corner_rows(region).index((c, y, z)))

    for c in range(3):
        for z in range(8):
            total = f_main[tile_rows(c * 8 + z), :]
            lines = [row_of(24 + c * 2, z), row_of(25 + c * 2, z), row_of(30 + c, z)]
            if z < 2 or z == 7:
                if z < 2:
                    total = total + vmain[tile_rows(33 + c * 2 + z), :]
                    low, high = (-1, -1), (1, -1)
                else:
                    total = total + vmain[tile_rows(39 + c), :]
                    low, high = (-1, 1), (1, 1)
                lines[0] = lines[0] + corner_row(low, c, 0, z)
                lines[1] = lines[1] + corner_row(low, c, 1, z)
                lines[2] = lines[2] + corner_row(high, c, 7, z)
            beside = jnp.where(sub == 0, lines[0], jnp.where(sub == 1, lines[1], jnp.where(sub == 7, lines[2], 0.0)))
            force[c, tile_rows(z), :] = total + beside

    for made in h_copies:
        made.wait_recv()
    for c in range(6):
        arrived[c, pl.ds(16, 52), :] = inbox[pl.ds(c, 52, stride=8), :]
    for made in started[waited + len(v_copies) :]:
        made.wait_send()


def deliver(state, force, arrived, state_hbm, force_hbm, arrived_hbm, sem):
    copies = [
        pltpu.make_async_copy(src, dst, sem.at[n])
        for n, (src, dst) in enumerate(((state, state_hbm), (force, force_hbm), (arrived, arrived_hbm)))
    ]
    for made in copies:
        made.start()
    for made in copies:
        made.wait()


def solution(mesh):
    sizes = tuple(mesh.shape[a] for a in ("gx", "gy", "gz"))

    def body(*refs):
        kernel(sizes, *refs)

    def local(pops, coarse_pops, interface, drop_vel, drop_frac, home, counts, dest):
        vmem = pl.BlockSpec(memory_space=pltpu.VMEM)
        anywhere = pl.BlockSpec(memory_space=pl.ANY)
        made = pl.pallas_call(
            body,
            out_shape=(
                pltpu.VMEM((19, 64, 128), f32),
                pltpu.VMEM((3, 64, 128), f32),
                pltpu.VMEM((6, 68, 128), f32),
            ),
            in_specs=[pl.BlockSpec(memory_space=pltpu.HBM)] * 8,
            out_specs=(vmem, vmem, vmem),
            scratch_shapes=[
                pltpu.VMEM((19, 64, 128), f32),
                pltpu.VMEM((19, 8, 8, 128), bf16),
                pltpu.VMEM((8, 8, 128), jnp.int32),
                pltpu.VMEM((3, 16, 128), f32),
                pltpu.VMEM((3, 16, 128), f32),
                pltpu.VMEM((16, 128), jnp.int32),
                pltpu.SMEM((BLOCKS,), jnp.int32),
                pltpu.SMEM((BLOCKS,), jnp.int32),
                pltpu.VMEM((19, 64, 128), f32),
                pltpu.VMEM((19, 64, 128), f32),
                pltpu.VMEM((2, POST_TILES * 8, 128), f32),
                pltpu.VMEM((2, POST_TILES * 8, 128), f32),
                pltpu.VMEM((ROWS, 128), f32),
                pltpu.VMEM((24 * 8, 128), f32),
                pltpu.VMEM((72, 128), f32),
                pltpu.VMEM((2, 72, 128), f32),
                pltpu.VMEM((ROWS, 256), bf16),
                pltpu.VMEM((ROWS, 256), bf16),
                pltpu.VMEM((384, WIDE), bf16),
                pltpu.VMEM((12, 16, 128), f32),
                pltpu.VMEM((3, 16, 128), jnp.int32),
                pltpu.VMEM((BLOCKS, U_TILES * 8, 128), f32),
                pltpu.VMEM((PAIRS, 192, 256), f32),
                pltpu.VMEM((ROWS, WIDE), bf16),
                pltpu.VMEM((ROWS, WIDE), bf16),
                pltpu.VMEM((ROWS, 128), f32),
                pltpu.VMEM((ROWS, 128), f32),
                pltpu.VMEM((24 * 8, 128), f32),
                pltpu.VMEM((24 * 8, 128), f32),
                pltpu.VMEM((72, 128), f32),
                pltpu.VMEM((2, 72, 128), f32),
                pltpu.VMEM((BLOCKS * 8, 128), f32),
                pltpu.VMEM((416, 128), f32),
                pltpu.VMEM((416, 128), f32),
                pltpu.SemaphoreType.DMA((N_MSG,)),
                pltpu.SemaphoreType.DMA((N_MSG,)),
                pltpu.SemaphoreType.DMA((8,)),
            ],
            compiler_params=pltpu.CompilerParams(
                collective_id=0, has_side_effects=True, vmem_limit_bytes=36 * 1024 * 1024
            ),
            name="channel",
        )(
            *(
                pltpu.with_memory_space_constraint(x, pltpu.HBM)
                for x in (pops.reshape(19, 64, 128), coarse_pops, interface, drop_vel, drop_frac, home, counts, dest)
            )
        )
        state, force, arrived = pl.pallas_call(
            deliver,
            out_shape=(
                jax.ShapeDtypeStruct((19, 64, 128), f32),
                jax.ShapeDtypeStruct((3, 64, 128), f32),
                jax.ShapeDtypeStruct((6, 68, 128), f32),
            ),
            in_specs=[vmem] * 3,
            out_specs=(anywhere,) * 3,
            scratch_shapes=[pltpu.SemaphoreType.DMA((3,))],
            compiler_params=pltpu.CompilerParams(vmem_limit_bytes=8 * 1024 * 1024),
            name="deliver",
        )(*made)
        return state.reshape(19, 8, 8, 128), force.reshape(3, 8, 8, 128), arrived

    return jax.shard_map(
        local,
        mesh=mesh,
        in_specs=(
            P(None, "gz", "gy", "gx"),
            P(None, "gz", "gy", "gx"),
            P("gz", "gy", "gx"),
            P(None, ("gx", "gy", "gz"), None),
            P(None, ("gx", "gy", "gz"), None),
            P(("gx", "gy", "gz"), None),
            P(("gx", "gy", "gz")),
            P(("gx", "gy", "gz")),
        ),
        out_specs=(
            P(None, "gz", "gy", "gx"),
            P(None, "gz", "gy", "gx"),
            P(None, ("gx", "gy", "gz"), None),
        ),
        check_vma=False,
    )
```

time: 60.4 us -> 50.1 us (0.83)
  Pallas kernels: 56.2 us -> 49.3 us
  local copies, waits for them, and re-layouts: 3.34 us -> 0 us
    pallas_call x1 -> x2, Pallas kernels: 56.2 us -> 49.3 us  [the longest x1 48.4 us: local(): pl.pallas_call(body, out_shape=(pltpu.VMEM((19, 64, 128), f32), pltpu.VME...]
    unnamed x7 -> x0, local copies, waits for them, and re-layouts: 3.34 us -> none
where the time goes in v2:
time: 50.1 us; the launch traced here: 50 us
  Pallas kernels  49.3 us (98%)
  between operations  0.64 us (1%)
    pallas_call x1, Pallas kernels, local(): pl.pallas_call(body, out_shape=(pltpu.VMEM((19, 64, 128), f32), pltpu.VME...  48.4 us

profile of v2, /device:TPU:1, one launch (start us, length us, event | category | flops | bytes accessed | tf_op | source)
XLA Modules:
  0.0 50.0 jit_solution(15340369945448051326)
XLA Ops:
  0.6 48.4 %channel.1 = (f32[19,64,128]{2,1,0:T(8,128)S(1)}, f32[3,64,128]{2,1,0:T(8,128)S(1)}, f32[6,68,128]{2,1,0:T(8,128)S(1)}) custom-call(f32[19,64,128]{2,1,0:T(8,128)} %bitcast.3, bf16[19,8,8,128]{3,2,1,0:T(8,128)(2,1)} %refs_1_.1, s32[8,8,128]{2,1,0:T(8,128)} %refs_2_.1, f32[3,16,128]{2,1,0:T(8,128)} %refs_3_.1, f32[3,16,128]{2,1,0:T(8,128)} %refs_4_.1, ...), custom_call_target="tpu_custom_call" | custom-call | tf_op jit(solution)/shard_map/channel/pallas_call | solution.py:649
  49.0 0.9 %deliver.1 = (f32[19,64,128]{2,1,0:T(8,128)}, f32[3,64,128]{2,1,0:T(8,128)}, f32[6,68,128]{2,1,0:T(8,128)}) custom-call(f32[19,64,128]{2,1,0:T(8,128)S(1)} %get-tuple-element.9.state, f32[3,64,128]{2,1,0:T(8,128)S(1)} %get-tuple-element.10.force, f32[6,68,128]{2,1,0:T(8,128)S(1)} %get-tuple-element.11.arrived), custom_call_target="tpu_custom_call" | custom-call | tf_op jit(solution)/shard_map/deliver/pallas_call | solution.py:707

commit v3 on v2

--- a/solution.py
+++ b/solution.py
@@ -51,6 +51,7 @@
 ROWS = 48 * 8
 all_dirs = [(x, y, z) for z in (-1, 0, 1) for y in (-1, 0, 1) for x in (-1, 0, 1) if (x, y, z) != (0, 0, 0)]
 far_first = sorted(all_dirs, key=lambda d: -abs(d[0]) - abs(d[1]) - abs(d[2]))
+near_dirs = [d for d in far_first if 0 in d]
 U_TILES = 19
 WIDE = 2048
 N_POST = 18
@@ -78,7 +79,7 @@
     state_out, force, arrived,
     pops, coarse, interface, drop_vel, drop_frac, home, counts, dest,
     posts, state_mid, psend, precv, vmain, vsend, pksend, pkrecv, va, vb, weights,
-    taps, homes, spread_weights, tmain, shi, slo, f_main, f_beyond, fsend, frecv, fpsend, fprecv, states, outbox, inbox,
+    taps, homes, spread_weights, tmain, partial, shi, slo, f_main, f_beyond, fsend, frecv, fpsend, fprecv, states, outbox, inbox,
     send_sem, recv_sem, in_sem,
 ):
     n_x, n_y, n_z = sizes
@@ -120,6 +121,10 @@
         made.start()
         started.append(made)
         return made
+
+    barrier = pltpu.get_barrier_semaphore()
+    for d in near_dirs:
+        pl.semaphore_signal(barrier, inc=1, device_id=device(d), device_id_type=pl.DeviceIdType.MESH)
 
     loads = []
     for n, (src, dst) in enumerate(
@@ -136,10 +141,6 @@
     ):
         loads.append(pltpu.make_async_copy(src, dst, in_sem.at[n]))
         loads[-1].start()
-    barrier = pltpu.get_barrier_semaphore()
-    for d in far_first:
-        pl.semaphore_signal(barrier, inc=1, device_id=device(d), device_id_type=pl.DeviceIdType.MESH)
-
     def macroscopic(values):
         plus = {i: values[i] + values[i + 1] for i in range(1, 19, 2)}
         minus = {i: values[i] - values[i + 1] for i in range(1, 19, 2)}
@@ -156,7 +157,7 @@
         return density, flow
 
     def collide(source):
-        @pl.loop(0, 8)
+        @pl.loop(0, 8, unroll=2)
         def _(z):
             rows = pl.ds(pl.multiple_of(z * 8, 8), 8)
             values = [source[i, rows, :] for i in range(19)]
@@ -185,8 +186,7 @@
                 put(i, even + odd)
                 put(i + 1, even - odd)
 
-    def send_posts(r):
-        copies = {}
+    def pack_posts(r):
         for number, (d, (first, count)) in enumerate(post_msgs.items()):
             layer = {a: (7 if d[a] == 1 else 0) for a in (1, 2)}
             if d in face_pops:
@@ -208,6 +208,10 @@
             else:
                 for k, i in enumerate(listed):
                     psend[r, tile_rows(first + k), :] = posts[i, pl.ds(layer[1], 8, stride=8), :]
+
+    def send_posts(r):
+        copies = {}
+        for number, (d, (first, count)) in enumerate(post_msgs.items()):
             part = pl.ds(first * 8, count * 8)
             copies[d] = copy(r * N_POST + number, psend.at[r, part], precv.at[r, part], d)
         return copies
@@ -348,10 +352,12 @@
     for made in loads[:3]:
         made.wait()
     collide(pops)
-    pl.semaphore_wait(barrier, len(all_dirs))
+    pack_posts(0)
+    pl.semaphore_wait(barrier, len(near_dirs))
     first_copies = send_posts(0)
     stream(0, first_copies, state_mid)
     collide(state_mid)
+    pack_posts(1)
     second_copies = send_posts(1)
     for made in loads[3:]:
         made.wait()
@@ -382,6 +388,7 @@
         return acc
 
     v_copies = []
+    v_near = []
     number = 2 * N_POST
     for n, region in enumerate(region_list):
         first, count = regions[region]
@@ -394,13 +401,13 @@
         pksend[tile_rows(n), :] = packed
         for side, dx in ((0, -1), (1, 1)):
             part = pl.ds(n * 8, 8)
-            v_copies.append(copy(number, pksend.at[part], pkrecv.at[side, part], (dx,) + region))
+            made = copy(number, pksend.at[part], pkrecv.at[side, part], (dx,) + region)
+            (v_near if region == (0, 0) else v_copies).append(made)
             number += 1
         if region != (0, 0):
             part = pl.ds((first - 24) * 8, count * 8)
-            v_copies.append(
-                copy(number, vsend.at[part], vmain.at[pl.ds(first * 8, count * 8)], (0,) + region)
-            )
+            made = copy(number, vsend.at[part], vmain.at[pl.ds(first * 8, count * 8)], (0,) + region)
+            (v_near if 0 in region else v_copies).append(made)
             number += 1
 
     def split_main(low, high):
@@ -421,14 +428,10 @@
         w_high = weights[pl.ds(0, 128), lanes]
         tmain[p] = jnp.dot(va[pl.ds(0, 192), :], jnp.concatenate([w_high, w_high], axis=0), preferred_element_type=f32)
 
-    waited = len(started) - len(v_copies)
+    waited = 2 * N_POST
     for made in started[:waited]:
         made.wait_send()
-    for made in v_copies:
-        made.wait_recv()
-    split_main(12, 24)
-    beyond = {}
-    for n, region in enumerate(region_list):
+    def unpack(n, region):
         first, count = regions[region]
         merged = jnp.where(outer_low, pkrecv[1, tile_rows(n), :], pkrecv[0, tile_rows(n), :])
         for g in range(0, count, GROUP):
@@ -438,26 +441,73 @@
             value = jnp.where(lane < 40, high_part, jnp.where(lane < 80, low_part, pltpu.roll(high_part, 80, 1)))
             for k in range(g, min(g + GROUP, count)):
                 beyond[first + k] = pltpu.roll(value, (-3 * (k - g)) % 128, 1) if k > g else value
-    beyond[47] = jnp.zeros((8, 128), f32)
-    for t in range(ROWS // 16):
-        vb[pl.ds(t * 16, 16), pl.ds(128, 128)] = jnp.concatenate([beyond[2 * t], beyond[2 * t + 1]], axis=0).astype(bf16)
+
+    def store_beyond(low, high):
+        for t in range(low, high):
+            vb[pl.ds(t * 16, 16), pl.ds(128, 128)] = jnp.concatenate([beyond[2 * t], beyond[2 * t + 1]], axis=0).astype(bf16)
+
+    beyond = {47: jnp.zeros((8, 128), f32)}
+    for made in v_near:
+        made.wait_recv()
+    split_main(12, 21)
+    unpack(region_list.index((0, 0)), (0, 0))
+    store_beyond(0, 12)
 
     @pl.loop(0, PAIRS, unroll=UNROLL)
     def _(p):
         pair_lanes = pl.ds(pl.multiple_of(p * 256, 256), 256)
         w_high = weights[pl.ds(0, 128), pair_lanes]
-        w_rest = weights[pl.ds(128, 256), pair_lanes]
-        t_main = tmain[p] + jnp.dot(vb[pl.ds(0, 192), :], w_rest, preferred_element_type=f32)
-        t_out = jnp.dot(
-            va[pl.ds(192, 192), :], jnp.concatenate([w_high, w_high], axis=0), preferred_element_type=f32
-        ) + jnp.dot(vb[pl.ds(192, 192), :], w_rest, preferred_element_type=f32)
+        t_main = tmain[p] + jnp.dot(
+            vb[pl.ds(0, 192), :], weights[pl.ds(128, 256), pair_lanes], preferred_element_type=f32
+        )
+        t_face = jnp.dot(
+            va[pl.ds(192, 144), :], jnp.concatenate([w_high, w_high], axis=0), preferred_element_type=f32
+        ) + jnp.dot(
+            vb[pl.ds(192, 144), pl.ds(0, 128)], weights[pl.ds(128, 128), pair_lanes], preferred_element_type=f32
+        )
+        for j in range(2):
+            b = 2 * p + j
+
+            def tile(t):
+                source, at = (t_main, t) if t < 24 else (t_face, t - 24)
+                return source[at * 8 : at * 8 + 8, j * 128 : (j + 1) * 128]
+
+            def u(t):
+                return spread_weights[b, tile_rows(t), :]
+
+            for c in range(3):
+                acc = tile(24 + c * 2) * u(8) + tile(25 + c * 2) * u(9) + tile(30 + c) * u(10)
+                acc = acc + tile(33 + c * 2) * u(11) + tile(34 + c * 2) * u(12) + tile(39 + c) * u(13)
+                other = tile(c * 8) * u(0)
+                for z in range(1, 8):
+                    other = other + tile(c * 8 + z) * u(z)
+                partial[b, tile_rows(c), :] = acc + other
+
+    for made in v_copies:
+        made.wait_recv()
+    split_main(21, 24)
+    for n, region in enumerate(region_list):
+        if region != (0, 0):
+            unpack(n, region)
+    store_beyond(12, 24)
+
+    @pl.loop(0, PAIRS, unroll=UNROLL)
+    def _(p):
+        pair_lanes = pl.ds(pl.multiple_of(p * 256, 256), 256)
+        w_high = weights[pl.ds(0, 128), pair_lanes]
+        t_side = jnp.dot(
+            vb[pl.ds(192, 144), pl.ds(128, 128)], weights[pl.ds(256, 128), pair_lanes], preferred_element_type=f32
+        )
+        t_corner = jnp.dot(
+            va[pl.ds(336, 48), :], jnp.concatenate([w_high, w_high], axis=0), preferred_element_type=f32
+        ) + jnp.dot(vb[pl.ds(336, 48), :], weights[pl.ds(128, 256), pair_lanes], preferred_element_type=f32)
         for j in range(2):
             b = 2 * p + j
             lanes = pl.ds(pl.multiple_of(p * 256 + j * 128, 128), 128)
             block = pl.ds(b, 1)
 
             def tile(t):
-                source, at = (t_main, t) if t < 24 else (t_out, t - 24)
+                source, at = (t_side, t - 24) if t < 42 else (t_corner, t - 42)
                 return source[at * 8 : at * 8 + 8, j * 128 : (j + 1) * 128]
 
             def u(t):
@@ -476,9 +526,7 @@
                     acc = acc + jnp.where((sub >> 2) == c, p42, 0.0)
                 else:
                     acc = acc + p43
-                other = tile(c * 8) * u(0)
-                for z in range(1, 8):
-                    other = other + tile(c * 8 + z) * u(z)
+                other = partial[b, tile_rows(c), :]
                 acc = acc + tile(24 + c * 2) * u(8) + tile(25 + c * 2) * u(9) + tile(30 + c) * u(10)
                 acc = acc + tile(33 + c * 2) * u(11) + tile(34 + c * 2) * u(12) + tile(39 + c) * u(13)
                 sampled = jnp.sum(acc + other, axis=0, keepdims=True)
@@ -534,11 +582,12 @@
     def over_droplets(source, weight):
         return lax.dot_general(source, weight, (((1,), (1,)), ((), ())), preferred_element_type=f32)
 
-    near = over_droplets(shi[...], weights[pl.ds(0, 256), :])
     last = over_droplets(slo[...], jnp.concatenate([weights[pl.ds(0, 128), :], weights[pl.ds(256, 128), :]], axis=0))
-    f_main[...] = near[:, 0:128] + near[:, 128:256] + last[:, 0:128]
     part_high = over_droplets(shi[...], weights[pl.ds(256, 128), :])
     f_beyond[...] = part_high + last[:, 128:256]
+    near = over_droplets(shi[pl.ds(192, 192), :], weights[pl.ds(0, 256), :])
+    f_main[pl.ds(192, 192), :] = near[:, 0:128] + near[:, 128:256] + last[192:384, 0:128]
+    f_main[pl.ds(0, 192), :] = last[0:192, 0:128]
     shifted = lane - 80
     spot = jnp.where(lane < 36, third, jnp.where((lane >= 80) & (lane < 116), (shifted * 171) >> 9, -1))
 
@@ -573,6 +622,9 @@
         h_copies.append(copy(number, outbox.at[part], inbox.at[part], d))
         number += 1
 
+    near = over_droplets(shi[pl.ds(0, 192), :], weights[pl.ds(0, 256), :])
+    f_main[pl.ds(0, 192), :] += near[:, 0:128] + near[:, 128:256]
+
     stay_rows = lax.broadcasted_iota(jnp.int32, (16, 128), 0)
     stays = jnp.zeros((16, 128), jnp.int32)
     for b in range(BLOCKS):
@@ -580,7 +632,7 @@
     for c in range(6):
         arrived[c, pl.ds(0, 16), :] = jnp.where(stays == 13, states[pl.ds(c, 16, stride=8), :], 0.0)
 
-    for made in started[waited : waited + len(v_copies)]:
+    for made in started[waited : waited + 26]:
         made.wait_send()
     for made in f_copies:
         made.wait_recv()
@@ -622,15 +674,14 @@
         made.wait_recv()
     for c in range(6):
         arrived[c, pl.ds(16, 52), :] = inbox[pl.ds(c, 52, stride=8), :]
-    for made in started[waited + len(v_copies) :]:
+    for made in started[waited + 26 :]:
         made.wait_send()
 
 
 def deliver(state, force, arrived, state_hbm, force_hbm, arrived_hbm, sem):
-    copies = [
-        pltpu.make_async_copy(src, dst, sem.at[n])
-        for n, (src, dst) in enumerate(((state, state_hbm), (force, force_hbm), (arrived, arrived_hbm)))
-    ]
+    pairs = [(state.at[pl.ds(i, min(4, 19 - i))], state_hbm.at[pl.ds(i, min(4, 19 - i))]) for i in range(0, 19, 4)]
+    pairs += [(arrived, arrived_hbm), (force, force_hbm)]
+    copies = [pltpu.make_async_copy(src, dst, sem.at[n]) for n, (src, dst) in enumerate(pairs)]
     for made in copies:
         made.start()
     for made in copies:
@@ -679,6 +730,7 @@
                 pltpu.VMEM((3, 16, 128), jnp.int32),
                 pltpu.VMEM((BLOCKS, U_TILES * 8, 128), f32),
                 pltpu.VMEM((PAIRS, 192, 256), f32),
+                pltpu.VMEM((BLOCKS, 24, 128), f32),
                 pltpu.VMEM((ROWS, WIDE), bf16),
                 pltpu.VMEM((ROWS, WIDE), bf16),
                 pltpu.VMEM((ROWS, 128), f32),
@@ -713,7 +765,7 @@
             ),
             in_specs=[vmem] * 3,
             out_specs=(anywhere,) * 3,
-            scratch_shapes=[pltpu.SemaphoreType.DMA((3,))],
+            scratch_shapes=[pltpu.SemaphoreType.DMA((7,))],
             compiler_params=pltpu.CompilerParams(vmem_limit_bytes=8 * 1024 * 1024),
             name="deliver",
         )(*made)

time: 50.1 us -> 49.4 us (0.986)
  Pallas kernels: 49.3 us -> 48.6 us
    pallas_call x1, Pallas kernels: 48.4 us -> 47.6 us  [local(): pl.pallas_call(body, out_shape=(pltpu.VMEM((19, 64, 128), f32), pltpu.VME...]
where the time goes in v3:
time: 49.4 us; the launch traced here: 49.2 us
  Pallas kernels  48.6 us (98%)
  between operations  0.64 us (1%)
    pallas_call x1, Pallas kernels, local(): pl.pallas_call(body, out_shape=(pltpu.VMEM((19, 64, 128), f32), pltpu.VME...  47.6 us

profile of v3, /device:TPU:1, one launch (start us, length us, event | category | flops | bytes accessed | tf_op | source)
XLA Modules:
  0.0 49.2 jit_solution(3978577117134108954)
XLA Ops:
  0.6 47.6 %channel.1 = (f32[19,64,128]{2,1,0:T(8,128)S(1)}, f32[3,64,128]{2,1,0:T(8,128)S(1)}, f32[6,68,128]{2,1,0:T(8,128)S(1)}) custom-call(f32[19,64,128]{2,1,0:T(8,128)} %bitcast.3, bf16[19,8,8,128]{3,2,1,0:T(8,128)(2,1)} %refs_1_.1, s32[8,8,128]{2,1,0:T(8,128)} %refs_2_.1, f32[3,16,128]{2,1,0:T(8,128)} %refs_3_.1, f32[3,16,128]{2,1,0:T(8,128)} %refs_4_.1, ...), custom_call_target="tpu_custom_call" | custom-call | tf_op jit(solution)/shard_map/channel/pallas_call | solution.py:700
  48.2 1.0 %deliver.1 = (f32[19,64,128]{2,1,0:T(8,128)}, f32[3,64,128]{2,1,0:T(8,128)}, f32[6,68,128]{2,1,0:T(8,128)}) custom-call(f32[19,64,128]{2,1,0:T(8,128)S(1)} %get-tuple-element.9.state, f32[3,64,128]{2,1,0:T(8,128)S(1)} %get-tuple-element.10.force, f32[6,68,128]{2,1,0:T(8,128)S(1)} %get-tuple-element.11.arrived), custom_call_target="tpu_custom_call" | custom-call | tf_op jit(solution)/shard_map/deliver/pallas_call | solution.py:759

commit v4 on v3

--- a/solution.py
+++ b/solution.py
@@ -186,8 +186,8 @@
                 put(i, even + odd)
                 put(i + 1, even - odd)
 
-    def pack_posts(r):
-        for number, (d, (first, count)) in enumerate(post_msgs.items()):
+    def pack_posts(r, part):
+        for d, (first, count) in list(post_msgs.items())[part]:
             layer = {a: (7 if d[a] == 1 else 0) for a in (1, 2)}
             if d in face_pops:
                 listed = face_pops[d]
@@ -209,12 +209,14 @@
                 for k, i in enumerate(listed):
                     psend[r, tile_rows(first + k), :] = posts[i, pl.ds(layer[1], 8, stride=8), :]
 
-    def send_posts(r):
-        copies = {}
-        for number, (d, (first, count)) in enumerate(post_msgs.items()):
-            part = pl.ds(first * 8, count * 8)
-            copies[d] = copy(r * N_POST + number, psend.at[r, part], precv.at[r, part], d)
-        return copies
+    edges, faces = slice(0, 12), slice(12, 18)
+
+    def send_posts(r, part):
+        for d, (first, count) in list(post_msgs.items())[part]:
+            rows = pl.ds(first * 8, count * 8)
+            post_copies[r].append(copy(len(started), psend.at[r, rows], precv.at[r, rows], d))
+
+    post_copies = ([], [])
 
     def pull(r, i):
         cx, cy, cz = lattice[i]
@@ -264,7 +266,7 @@
         return out
 
     def stream(r, copies, into):
-        for made in copies.values():
+        for made in copies:
             made.wait_recv()
         for i in range(19):
             out = pull(r, i)
@@ -352,19 +354,23 @@
     for made in loads[:3]:
         made.wait()
     collide(pops)
-    pack_posts(0)
+    pack_posts(0, edges)
+    pack_posts(0, faces)
     pl.semaphore_wait(barrier, len(near_dirs))
-    first_copies = send_posts(0)
-    stream(0, first_copies, state_mid)
+    send_posts(0, edges)
+    send_posts(0, faces)
+    stream(0, post_copies[0], state_mid)
     collide(state_mid)
-    pack_posts(1)
-    second_copies = send_posts(1)
+    pack_posts(1, edges)
+    send_posts(1, edges)
+    pack_posts(1, faces)
+    send_posts(1, faces)
     for made in loads[3:]:
         made.wait()
     prepare()
     build_x_weights()
     build_yz_weights()
-    stream(1, second_copies, state_out)
+    stream(1, post_copies[1], state_out)
 
     for z in range(8):
         values = [state_out[i, tile_rows(z), :] for i in range(19)]
@@ -387,9 +393,7 @@
             acc = jnp.where(sub == r, vmain[pl.ds(c * 64 + z * 8 + y, 1), :], acc)
         return acc
 
-    v_copies = []
-    v_near = []
-    number = 2 * N_POST
+    v_copies = {1: [], 2: [], 3: []}
     for n, region in enumerate(region_list):
         first, count = regions[region]
         packed = jnp.zeros((8, 128), f32)
@@ -401,14 +405,12 @@
         pksend[tile_rows(n), :] = packed
         for side, dx in ((0, -1), (1, 1)):
             part = pl.ds(n * 8, 8)
-            made = copy(number, pksend.at[part], pkrecv.at[side, part], (dx,) + region)
-            (v_near if region == (0, 0) else v_copies).append(made)
-            number += 1
+            made = copy(len(started), pksend.at[part], pkrecv.at[side, part], (dx,) + region)
+            v_copies[1 + abs(region[0]) + abs(region[1])].append(made)
         if region != (0, 0):
             part = pl.ds((first - 24) * 8, count * 8)
-            made = copy(number, vsend.at[part], vmain.at[pl.ds(first * 8, count * 8)], (0,) + region)
-            (v_near if 0 in region else v_copies).append(made)
-            number += 1
+            made = copy(len(started), vsend.at[part], vmain.at[pl.ds(first * 8, count * 8)], (0,) + region)
+            v_copies[abs(region[0]) + abs(region[1])].append(made)
 
     def split_main(low, high):
         for t in range(low, high):
@@ -447,7 +449,7 @@
             vb[pl.ds(t * 16, 16), pl.ds(128, 128)] = jnp.concatenate([beyond[2 * t], beyond[2 * t + 1]], axis=0).astype(bf16)
 
     beyond = {47: jnp.zeros((8, 128), f32)}
-    for made in v_near:
+    for made in v_copies[1]:
         made.wait_recv()
     split_main(12, 21)
     unpack(region_list.index((0, 0)), (0, 0))
@@ -483,13 +485,24 @@
                     other = other + tile(c * 8 + z) * u(z)
                 partial[b, tile_rows(c), :] = acc + other
 
-    for made in v_copies:
+    def corner_terms(tile, u):
+        p42 = tile(42) * u(14)
+        p43 = tile(43) * u(15)
+        p445 = tile(44) * u(16) + tile(45) * u(17)
+        p46 = tile(46) * u(18)
+        terms = []
+        for c in range(3):
+            acc = jnp.where((sub >> 1) == c, p445, 0.0) + jnp.where(sub == c, p46, 0.0)
+            terms.append(acc + (jnp.where((sub >> 2) == c, p42, 0.0) if c < 2 else p43))
+        return terms
+
+    for made in v_copies[2]:
         made.wait_recv()
     split_main(21, 24)
     for n, region in enumerate(region_list):
-        if region != (0, 0):
+        if abs(region[0]) + abs(region[1]) == 1:
             unpack(n, region)
-    store_beyond(12, 24)
+    store_beyond(12, 21)
 
     @pl.loop(0, PAIRS, unroll=UNROLL)
     def _(p):
@@ -500,36 +513,55 @@
         )
         t_corner = jnp.dot(
             va[pl.ds(336, 48), :], jnp.concatenate([w_high, w_high], axis=0), preferred_element_type=f32
-        ) + jnp.dot(vb[pl.ds(336, 48), :], weights[pl.ds(128, 256), pair_lanes], preferred_element_type=f32)
+        ) + jnp.dot(
+            vb[pl.ds(336, 48), pl.ds(0, 128)], weights[pl.ds(128, 128), pair_lanes], preferred_element_type=f32
+        )
+        for j in range(2):
+            b = 2 * p + j
+
+            def tile(t):
+                source, at = (t_side, t - 24) if t < 42 else (t_corner, t - 42)
+                return source[at * 8 : at * 8 + 8, j * 128 : (j + 1) * 128]
+
+            def u(t):
+                return spread_weights[b, tile_rows(t), :]
+
+            for c, acc in enumerate(corner_terms(tile, u)):
+                acc = acc + tile(24 + c * 2) * u(8) + tile(25 + c * 2) * u(9) + tile(30 + c) * u(10)
+                acc = acc + tile(33 + c * 2) * u(11) + tile(34 + c * 2) * u(12) + tile(39 + c) * u(13)
+                partial[b, tile_rows(c), :] += acc
+
+    for made in v_copies[3]:
+        made.wait_recv()
+    for n, region in enumerate(region_list):
+        if abs(region[0]) + abs(region[1]) == 2:
+            unpack(n, region)
+    store_beyond(21, 24)
+
+    @pl.loop(0, PAIRS, unroll=UNROLL)
+    def _(p):
+        pair_lanes = pl.ds(pl.multiple_of(p * 256, 256), 256)
+        t_corner = jnp.dot(
+            vb[pl.ds(336, 48), pl.ds(128, 128)], weights[pl.ds(256, 128), pair_lanes], preferred_element_type=f32
+        )
         for j in range(2):
             b = 2 * p + j
             lanes = pl.ds(pl.multiple_of(p * 256 + j * 128, 128), 128)
             block = pl.ds(b, 1)
 
             def tile(t):
-                source, at = (t_side, t - 24) if t < 42 else (t_corner, t - 42)
-                return source[at * 8 : at * 8 + 8, j * 128 : (j + 1) * 128]
+                return t_corner[(t - 42) * 8 : (t - 41) * 8, j * 128 : (j + 1) * 128]
 
             def u(t):
                 return spread_weights[b, tile_rows(t), :]
 
-            p42 = tile(42) * u(14)
-            p43 = tile(43) * u(15)
-            p445 = tile(44) * u(16) + tile(45) * u(17)
-            p46 = tile(46) * u(18)
+            terms = corner_terms(tile, u)
             alive = lax.broadcasted_iota(jnp.int32, (1, 128), 1) < counts[b]
             pushes = []
             rows = []
             for c in range(3):
-                acc = jnp.where((sub >> 1) == c, p445, 0.0) + jnp.where(sub == c, p46, 0.0)
-                if c < 2:
-                    acc = acc + jnp.where((sub >> 2) == c, p42, 0.0)
-                else:
-                    acc = acc + p43
-                other = partial[b, tile_rows(c), :]
-                acc = acc + tile(24 + c * 2) * u(8) + tile(25 + c * 2) * u(9) + tile(30 + c) * u(10)
-                acc = acc + tile(33 + c * 2) * u(11) + tile(34 + c * 2) * u(12) + tile(39 + c) * u(13)
-                sampled = jnp.sum(acc + other, axis=0, keepdims=True)
+                acc = terms[c] + partial[b, tile_rows(c), :]
+                sampled = jnp.sum(acc, axis=0, keepdims=True)
                 speed = drop_vel[c, block, :]
                 moved = speed + relax * (sampled - speed)
                 pushes.append(jnp.where(alive, couple * (moved - sampled), 0.0))
@@ -579,21 +611,44 @@
         + jnp.dot(chosen, part_1, preferred_element_type=f32)
         + jnp.dot(chosen, part_2, preferred_element_type=f32)
     )
+    h_copies = []
+
+    def hand_over(hops):
+        for d in far_first:
+            if abs(d[0]) + abs(d[1]) + abs(d[2]) == hops:
+                part = pl.ds(all_dirs.index(d) * 16, 16)
+                h_copies.append(copy(len(started), outbox.at[part], inbox.at[part], d))
+
+    hand_over(3)
+
     def over_droplets(source, weight):
         return lax.dot_general(source, weight, (((1,), (1,)), ((), ())), preferred_element_type=f32)
 
-    last = over_droplets(slo[...], jnp.concatenate([weights[pl.ds(0, 128), :], weights[pl.ds(256, 128), :]], axis=0))
-    part_high = over_droplets(shi[...], weights[pl.ds(256, 128), :])
-    f_beyond[...] = part_high + last[:, 128:256]
-    near = over_droplets(shi[pl.ds(192, 192), :], weights[pl.ds(0, 256), :])
-    f_main[pl.ds(192, 192), :] = near[:, 0:128] + near[:, 128:256] + last[192:384, 0:128]
-    f_main[pl.ds(0, 192), :] = last[0:192, 0:128]
     shifted = lane - 80
     spot = jnp.where(lane < 36, third, jnp.where((lane >= 80) & (lane < 116), (shifted * 171) >> 9, -1))
 
     f_copies = []
+    thirds = weights[pl.ds(256, 128), :]
+
+    def spread_rows(low, count):
+        rows = pl.ds(low, count)
+        near = over_droplets(shi[rows, :], weights[pl.ds(0, 256), :])
+        last = over_droplets(slo[rows, :], jnp.concatenate([weights[pl.ds(0, 128), :], thirds], axis=0))
+        f_beyond[rows, :] = over_droplets(shi[rows, :], thirds) + last[:, 128:256]
+        f_main[rows, :] = near[:, 0:128] + near[:, 128:256] + last[:, 0:128]
+
+    spread_rows(336, 48)
+    done = 2
     for n, region in enumerate(region_list):
         first, count = regions[region]
+        if abs(region[0]) + abs(region[1]) < done:
+            hand_over(done)
+            done -= 1
+            if done == 1:
+                spread_rows(192, 144)
+            else:
+                own = pl.ds(0, 192)
+                f_beyond[own, :] = over_droplets(shi[own, :], thirds) + over_droplets(slo[own, :], thirds)
         packed = None
         for g in range(0, count, GROUP):
             value = jnp.zeros((8, 128), f32)
@@ -609,21 +664,14 @@
         back = (-region[0], -region[1])
         for side, dx in ((0, -1), (1, 1)):
             part = pl.ds(n * 8, 8)
-            f_copies.append(copy(number, fpsend.at[part], fprecv.at[side, part], (-dx,) + back))
-            number += 1
+            f_copies.append(copy(len(started), fpsend.at[part], fprecv.at[side, part], (-dx,) + back))
         if region != (0, 0):
             part = pl.ds((first - 24) * 8, count * 8)
-            f_copies.append(copy(number, fsend.at[part], frecv.at[part], (0,) + back))
-            number += 1
-
-    h_copies = []
-    for d in far_first:
-        part = pl.ds(all_dirs.index(d) * 16, 16)
-        h_copies.append(copy(number, outbox.at[part], inbox.at[part], d))
-        number += 1
-
-    near = over_droplets(shi[pl.ds(0, 192), :], weights[pl.ds(0, 256), :])
-    f_main[pl.ds(0, 192), :] += near[:, 0:128] + near[:, 128:256]
+            f_copies.append(copy(len(started), fsend.at[part], frecv.at[part], (0,) + back))
+
+    near = over_droplets(shi[own, :], weights[pl.ds(0, 256), :])
+    last = over_droplets(slo[own, :], weights[pl.ds(0, 128), :])
+    f_main[own, :] = near[:, 0:128] + near[:, 128:256] + last
 
     stay_rows = lax.broadcasted_iota(jnp.int32, (16, 128), 0)
     stays = jnp.zeros((16, 128), jnp.int32)

time: 49.4 us -> 49.4 us (level)
  no operation moved by 1% of the time
where the time goes in v4:
time: 49.4 us; the launch traced here: 49.2 us
  Pallas kernels  48.6 us (98%)
  between operations  0.64 us (1%)
    pallas_call x1, Pallas kernels, local(): pl.pallas_call(body, out_shape=(pltpu.VMEM((19, 64, 128), f32), pltpu.VME...  47.6 us

profile of v4, /device:TPU:1, one launch (start us, length us, event | category | flops | bytes accessed | tf_op | source)
XLA Modules:
  0.0 49.2 jit_solution(17914389579355523035)
XLA Ops:
  0.6 47.6 %channel.1 = (f32[19,64,128]{2,1,0:T(8,128)S(1)}, f32[3,64,128]{2,1,0:T(8,128)S(1)}, f32[6,68,128]{2,1,0:T(8,128)S(1)}) custom-call(f32[19,64,128]{2,1,0:T(8,128)} %bitcast.3, bf16[19,8,8,128]{3,2,1,0:T(8,128)(2,1)} %refs_1_.1, s32[8,8,128]{2,1,0:T(8,128)} %refs_2_.1, f32[3,16,128]{2,1,0:T(8,128)} %refs_3_.1, f32[3,16,128]{2,1,0:T(8,128)} %refs_4_.1, ...), custom_call_target="tpu_custom_call" | custom-call | tf_op jit(solution)/shard_map/channel/pallas_call | solution.py:748
  48.3 1.0 %deliver.1 = (f32[19,64,128]{2,1,0:T(8,128)}, f32[3,64,128]{2,1,0:T(8,128)}, f32[6,68,128]{2,1,0:T(8,128)}) custom-call(f32[19,64,128]{2,1,0:T(8,128)S(1)} %get-tuple-element.9.state, f32[3,64,128]{2,1,0:T(8,128)S(1)} %get-tuple-element.10.force, f32[6,68,128]{2,1,0:T(8,128)S(1)} %get-tuple-element.11.arrived), custom_call_target="tpu_custom_call" | custom-call | tf_op jit(solution)/shard_map/deliver/pallas_call | solution.py:807

commit v5 on v4

--- a/solution.py
+++ b/solution.py
@@ -637,16 +637,14 @@
         f_beyond[rows, :] = over_droplets(shi[rows, :], thirds) + last[:, 128:256]
         f_main[rows, :] = near[:, 0:128] + near[:, 128:256] + last[:, 0:128]
 
-    spread_rows(336, 48)
+    spread_rows(192, 192)
     done = 2
     for n, region in enumerate(region_list):
         first, count = regions[region]
         if abs(region[0]) + abs(region[1]) < done:
             hand_over(done)
             done -= 1
-            if done == 1:
-                spread_rows(192, 144)
-            else:
+            if done == 0:
                 own = pl.ds(0, 192)
                 f_beyond[own, :] = over_droplets(shi[own, :], thirds) + over_droplets(slo[own, :], thirds)
         packed = None

time: 49.4 us -> 49.2 us (level)
  no operation moved by 1% of the time
where the time goes in v5:
time: 49.2 us; the launch traced here: 49 us
  Pallas kernels  48.4 us (98%)
  between operations  0.64 us (1%)
    pallas_call x1, Pallas kernels, local(): pl.pallas_call(body, out_shape=(pltpu.VMEM((19, 64, 128), f32), pltpu.VME...  47.4 us

profile of v5, /device:TPU:1, one launch (start us, length us, event | category | flops | bytes accessed | tf_op | source)
XLA Modules:
  0.0 49.0 jit_solution(18267048331644136388)
XLA Ops:
  0.6 47.4 %channel.1 = (f32[19,64,128]{2,1,0:T(8,128)S(1)}, f32[3,64,128]{2,1,0:T(8,128)S(1)}, f32[6,68,128]{2,1,0:T(8,128)S(1)}) custom-call(f32[19,64,128]{2,1,0:T(8,128)} %bitcast.3, bf16[19,8,8,128]{3,2,1,0:T(8,128)(2,1)} %refs_1_.1, s32[8,8,128]{2,1,0:T(8,128)} %refs_2_.1, f32[3,16,128]{2,1,0:T(8,128)} %refs_3_.1, f32[3,16,128]{2,1,0:T(8,128)} %refs_4_.1, ...), custom_call_target="tpu_custom_call" | custom-call | tf_op jit(solution)/shard_map/channel/pallas_call | solution.py:746
  48.0 1.0 %deliver.1 = (f32[19,64,128]{2,1,0:T(8,128)}, f32[3,64,128]{2,1,0:T(8,128)}, f32[6,68,128]{2,1,0:T(8,128)}) custom-call(f32[19,64,128]{2,1,0:T(8,128)S(1)} %get-tuple-element.9.state, f32[3,64,128]{2,1,0:T(8,128)S(1)} %get-tuple-element.10.force, f32[6,68,128]{2,1,0:T(8,128)S(1)} %get-tuple-element.11.arrived), custom_call_target="tpu_custom_call" | custom-call | tf_op jit(solution)/shard_map/deliver/pallas_call | solution.py:805
